TPU v7x, 128 devices: a whole 4x4x4 slice. The times are simulated.
128 devices in a mesh: pts: 32 (over z, x, core), grp: 4 (over y).
Axes of the slice: x: 4, y: 4, z: 4, core: 2. Of those that a mesh axis runs over, the one named last changes fastest.
Arguments:
- points: bfloat16 [262144, 256], P(('pts', 'grp')), may hold values from -6 to 6
- rot_dest: int32 [4096], replicated, may hold values from 0 to 4095, as said below
- block_order: int32 [32, 32], P('pts'), may hold values from 0 to 31, each once within a row
- ball_sizes: int32 [32, 8], P('pts'), may hold values from 1 to 8, 32 in all within a row
- fine_gain: float32 [3, 256], replicated, may hold values from 0.1 to 1.9
- fine_qkv: bfloat16 [3, 256, 768], replicated, may hold values from -0.375 to 0.375
- fine_out: bfloat16 [3, 256, 256], replicated, may hold values from -0.375 to 0.375
- pool_weight: bfloat16 [1024, 512], replicated, may hold values from -0.1875 to 0.1875
- coarse_gain: float32 [512], replicated, may hold values from 0.1 to 1.9
- coarse_qkv: bfloat16 [512, 1536], replicated, may hold values from -0.25 to 0.25
- coarse_out: bfloat16 [512, 512], replicated, may hold values from -0.25 to 0.25
- unpool_weight: bfloat16 [512, 1024], replicated, may hold values from -0.25 to 0.25
Outputs:
- refined: bfloat16 [262144, 256], P(('pts', 'grp'))
- coarse: bfloat16 [65536, 512], P(('pts', 'grp'))
Inputs may be any that keep to these rules, and one draw needn't show every extreme that they name: A permutation of the sub-blocks. Sub-block s lies on device s // 32 and goes to the device that holds position rot_dest[s]; that device has the same index along grp, and every device sends exactly one sub-block to each device along pts. `block_order`: each row is a permutation. `ball_sizes`: each row sums to 32.
All inputs are finite; a program needn't handle non-finite values.
Results may differ from a plain program's by a relative error of at most 0.012.
Values may be sent and summed in bfloat16 or wider, within the bound.
No kernel may reach another device: no remote copies, remote signals or barrier semaphores. Data moves between devices by JAX's collectives and lax.ppermute only.
A program may use at most 128 MiB of HBM per device.

v0:
```python
import functools
import math

import jax
import jax.numpy as jnp
from jax import lax
from jax.experimental import pallas as pl
from jax.experimental.pallas import tpu as pltpu
from jax.sharding import PartitionSpec as P

F32, BF16 = jnp.float32, jnp.bfloat16
HEADS = 8
BALL = 256
SUB = 64
CBLK = 64
MOST_BALL = 8
WIDTH = 256
CWIDTH = 512
SUBS = 32
POOL = 16
LOG2E = 1.4426950408889634
NT = (((1,), (1,)), ((), ()))
TN = (((0,), (0,)), ((), ()))
VMEM = pl.BlockSpec(memory_space=pltpu.VMEM)
SMEM = pl.BlockSpec(memory_space=pltpu.SMEM)


def dot(a, b, dims=None):
    if dims is None:
        return jnp.dot(a, b, preferred_element_type=F32)
    return lax.dot_general(a, b, dims, preferred_element_type=F32)


def norm(x, gain):
    return (x * lax.rsqrt(jnp.mean(x * x, axis=-1, keepdims=True) + 1e-6) * gain).astype(BF16)


def head_masks():
    lane = lax.broadcasted_iota(jnp.int32, (1, 128), 1) // 32
    return [(lane == i).astype(F32).astype(BF16) for i in range(4)]


def fine_mixed(h, wqkv, wvt, wo, masks):
    q = (dot(h, wqkv[:, :WIDTH]) * (LOG2E / math.sqrt(32.0))).astype(BF16)
    k = dot(h, wqkv[:, WIDTH : 2 * WIDTH]).astype(BF16)
    vt = dot(wvt, h, NT).astype(BF16)
    ones = jnp.ones((16, BALL), BF16)
    heads = []
    for g in range(2):
        kg = k[:, 128 * g : 128 * g + 128]
        qg = q[:, 128 * g : 128 * g + 128]
        kc = jnp.concatenate([kg * masks[i] for i in range(4)], axis=0)
        sc = dot(kc, qg, NT)
        for i in range(4):
            head = 4 * g + i
            s = sc[BALL * i : BALL * (i + 1)]
            top = jnp.max(s, axis=0, keepdims=True)
            p = jnp.exp2(s - top).astype(BF16)
            o = dot(jnp.concatenate([vt[32 * head : 32 * head + 32], ones], axis=0), p)
            heads.append((o[:32] * (1.0 / o[32:33])).astype(BF16))
    return dot(jnp.concatenate(heads, axis=0), wo, TN)


def gathered(ref, table, b):
    return jnp.concatenate([ref[table[4 * b + i]] for i in range(4)], axis=0)


def first_kernel(tables, x_ref, gain_ref, wqkv_ref, wo_ref, out_ref, wvt_ref):
    wvt_ref[...] = wqkv_ref[:, 2 * WIDTH :].T
    masks = head_masks()

    def ball(b, carry):
        x = x_ref[pl.ds(4 * b, 4)].reshape(BALL, WIDTH).astype(F32)
        h = norm(x, gain_ref[...])
        y = (x + fine_mixed(h, wqkv_ref[...], wvt_ref[...], wo_ref[...], masks)).astype(BF16)
        for i in range(4):
            out_ref[tables[0, 4 * b + i]] = y[SUB * i : SUB * (i + 1)]
        return carry

    lax.fori_loop(0, SUBS // 4, ball, 0)


def second_kernel(
    tables, x_ref, gain_ref, wqkv_ref, wo_ref, pool_ref, out_ref, pooled_ref, wvt_ref, wide_ref
):
    wvt_ref[...] = wqkv_ref[:, 2 * WIDTH :].T
    masks = head_masks()

    def ball(b, carry):
        x = jnp.concatenate([x_ref[tables[1, 4 * b + i]] for i in range(4)], axis=0).astype(F32)
        h = norm(x, gain_ref[...])
        y = (x + fine_mixed(h, wqkv_ref[...], wvt_ref[...], wo_ref[...], masks)).astype(BF16)
        out_ref[b] = y
        wide = y.astype(F32)
        for c in range(2):
            wide_ref[c] = wide[:, 128 * c : 128 * c + 128]
        rows = jnp.concatenate(
            [wide_ref[c, pl.ds(j, BALL // 4, stride=4)] for j in range(4) for c in range(2)],
            axis=1,
        ).astype(BF16)
        pooled = dot(rows, pool_ref[...]).astype(BF16)
        for i in range(4):
            pooled_ref[tables[1, 4 * b + i]] = pooled[POOL * i : POOL * (i + 1)]
        return carry

    lax.fori_loop(0, SUBS // 4, ball, 0)


def third_kernel(
    tables, x_ref, coarse_ref, gain_ref, wqkv_ref, wo_ref, unpool_ref, out_ref, wvt_ref, wide_ref
):
    wvt_ref[...] = wqkv_ref[:, 2 * WIDTH :].T
    masks = head_masks()

    def ball(b, carry):
        coarse = jnp.concatenate([coarse_ref[tables[1, 4 * b + i]] for i in range(4)], axis=0)
        lifted = dot(coarse, unpool_ref[...])
        for j in range(4):
            for c in range(2):
                at = WIDTH * j + 128 * c
                wide_ref[c, pl.ds(j, BALL // 4, stride=4)] = lifted[:, at : at + 128]
        x = x_ref[b].astype(F32) + jnp.concatenate([wide_ref[0], wide_ref[1]], axis=1)
        x = x.astype(BF16).astype(F32)
        h = norm(x, gain_ref[...])
        y = (x + fine_mixed(h, wqkv_ref[...], wvt_ref[...], wo_ref[...], masks)).astype(BF16)
        for i in range(4):
            out_ref[tables[1, 4 * b + i]] = y[SUB * i : SUB * (i + 1)]
        return carry

    lax.fori_loop(0, SUBS // 4, ball, 0)


def ordered_kernel(tables, x_ref, out_ref):
    for s in range(SUBS):
        out_ref[s] = x_ref[tables[0, s]]


def coarse_start_kernel(tables, pieces_ref, gain_ref, pooled_ref, normed_ref):
    for s in range(SUBS):
        piece = pieces_ref[tables[0, s]]
        pooled_ref[POOL * s : POOL * (s + 1)] = piece
    normed_ref[...] = norm(pooled_ref[...].astype(F32), gain_ref[...])


def project_kernel(*refs):
    count = (len(refs) - 1) // 2
    w_ref = refs[count]
    for x_ref, out_ref in zip(refs[:count], refs[count + 1 :]):
        out_ref[...] = dot(x_ref[...], w_ref[...]).astype(BF16)


def coarse_kernel(
    tables,
    blocks,
    counts,
    pooled_ref,
    own_ref,
    left_ref,
    right_ref,
    far_a_ref,
    far_b_ref,
    wkv_ref,
    wo_ref,
    coarse_ref,
    sent_ref,
    kv_ref,
    att_ref,
    *,
    groups,
):
    me = tables[2, 0]
    rows = CWIDTH
    for step, ref in ((0, own_ref), (groups - 1, left_ref), (1, right_ref)):
        at = pl.multiple_of(lax.rem(me + step, groups) * rows, rows)
        kv_ref[pl.ds(at, rows)] = ref[:, ref.shape[1] - 2 * CWIDTH :]
    at = pl.multiple_of(lax.rem(me + 2, groups) * rows, rows)
    half = rows // 2
    kv_ref[pl.ds(at, half)] = dot(far_a_ref[...], wkv_ref[...]).astype(BF16)
    kv_ref[pl.ds(at + half, half)] = dot(far_b_ref[...], wkv_ref[...]).astype(BF16)
    size = 64
    lanes = lax.broadcasted_iota(jnp.int32, (1, 256), 1) // size
    keep = [(lanes == i).astype(F32) for i in range(4)]
    keep_low = [m.astype(BF16) for m in keep]
    member = lax.broadcasted_iota(jnp.int32, (1, MOST_BALL * CBLK), 1) // CBLK

    def block(b, carry):
        valid = member < counts[b]
        starts = [pl.multiple_of(blocks[b * MOST_BALL + m] * CBLK, CBLK) for m in range(MOST_BALL)]
        begin = pl.multiple_of(b * CBLK, CBLK)
        for g in range(2):
            q = own_ref[pl.ds(begin, CBLK), 256 * g : 256 * g + 256]
            spread = jnp.concatenate([q * keep_low[i] for i in range(4)], axis=0)
            keys = jnp.concatenate(
                [kv_ref[pl.ds(s, CBLK), 256 * g : 256 * g + 256] for s in starts], axis=0
            )
            vals = jnp.concatenate(
                [kv_ref[pl.ds(s, CBLK), CWIDTH + 256 * g : CWIDTH + 256 * g + 256] for s in starts],
                axis=0,
            )
            scores = jnp.where(valid, dot(spread, keys, NT) * (LOG2E / 8.0), -jnp.inf)
            top = jnp.max(scores, axis=-1, keepdims=True)
            expo = jnp.exp2(scores - top)
            probs = (expo * (1.0 / jnp.sum(expo, axis=-1, keepdims=True))).astype(BF16)
            out = dot(probs, vals)
            total = sum(out[CBLK * i : CBLK * (i + 1)] * keep[i] for i in range(4))
            att_ref[pl.ds(begin, CBLK), 256 * g : 256 * g + 256] = total.astype(BF16)
        return carry

    lax.fori_loop(0, rows // CBLK, block, 0)
    result = (pooled_ref[...].astype(F32) + dot(att_ref[...], wo_ref[...])).astype(BF16)
    coarse_ref[...] = result
    for s in range(SUBS):
        sent_ref[tables[0, s]] = result[POOL * s : POOL * (s + 1)]


def call(kernel, outs, scratch, args, tables=1, flops=0, exps=0, name=None):
    size = sum(a.size * a.dtype.itemsize for a in args)
    return pl.pallas_call(
        kernel,
        out_shape=outs,
        in_specs=[SMEM] * tables + [VMEM] * (len(args) - tables),
        out_specs=jax.tree.map(lambda _: VMEM, outs),
        scratch_shapes=scratch,
        name=name,
        cost_estimate=pl.CostEstimate(flops=flops, bytes_accessed=2 * size, transcendentals=exps),
    )(*args)


def shaped(*shape):
    return jax.ShapeDtypeStruct(shape, BF16)


def exchange(pieces):
    return lax.all_to_all(pieces, "pts", split_axis=0, concat_axis=0, tiled=True)


def tables_of(rot_dest):
    points, groups = lax.axis_size("pts"), lax.axis_size("grp")
    group = lax.axis_index("grp")
    device = lax.axis_index("pts") * groups + group
    target = lax.dynamic_slice_in_dim(rot_dest, device * SUBS, SUBS) // SUBS // groups
    mine = lax.dynamic_index_in_dim(rot_dest.reshape(points, groups, SUBS), group, 1, False)
    slot = mine - device * SUBS
    source = jnp.arange(points, dtype=jnp.int32)
    hit = slot[None] == jnp.arange(SUBS, dtype=jnp.int32)[:, None, None]
    place = jnp.sum(jnp.where(hit, source[None, :, None], 0), axis=(1, 2))
    return jnp.stack([target, place, jnp.broadcast_to(group, (SUBS,))]).astype(jnp.int32)


def ball_table(order, sizes, count):
    total = order.shape[0]
    before = jnp.arange(sizes.shape[0])
    ends = jnp.sum(jnp.where(before[None, :] <= before[:, None], sizes[None, :], 0), axis=1)
    starts = ends - sizes
    marks = jnp.arange(total, dtype=jnp.int32)
    mine = lax.axis_index("grp") * count + jnp.arange(count, dtype=jnp.int32)
    where = jnp.sum(jnp.where(order[None, :] == mine[:, None], marks[None, :], 0), axis=1)
    inside = (starts[None, :] <= where[:, None]) & (where[:, None] < ends[None, :])
    first = jnp.sum(jnp.where(inside, starts[None, :], 0), axis=1)
    length = jnp.sum(jnp.where(inside, sizes[None, :], 0), axis=1)
    slots = jnp.arange(MOST_BALL, dtype=jnp.int32)
    place = jnp.minimum(first[:, None] + slots[None, :], total - 1)
    members = jnp.sum(
        jnp.where(place[:, :, None] == marks[None, None, :], order[None, None, :], 0), axis=2
    )
    return members.reshape(-1).astype(jnp.int32), length.astype(jnp.int32)


def body(
    points,
    rot_dest,
    block_order,
    ball_sizes,
    fine_gain,
    fine_qkv,
    fine_out,
    pool_weight,
    coarse_gain,
    coarse_qkv,
    coarse_out,
    unpool_weight,
):
    rows, width = points.shape
    groups = lax.axis_size("grp")
    crows = rows // 4
    tables = tables_of(rot_dest)
    members, lengths = ball_table(block_order[0], ball_sizes[0], crows // CBLK)
    gains = [fine_gain[j : j + 1] for j in range(3)]
    turn = pltpu.VMEM((width, width), BF16)
    wide = pltpu.VMEM((2, BALL, 128), F32)
    cost = dict(flops=5 * 10**9, exps=4 * 10**6)

    sent = call(
        first_kernel,
        shaped(SUBS, SUB, width),
        [turn],
        (tables, points.reshape(SUBS, SUB, width), gains[0], fine_qkv[0], fine_out[0]),
        name="first_layer",
        **cost,
    )
    arrived = exchange(sent)
    second, pieces = call(
        second_kernel,
        (shaped(SUBS // 4, BALL, width), shaped(SUBS, POOL, CWIDTH)),
        [turn, wide],
        (tables, arrived, gains[1], fine_qkv[1], fine_out[1], pool_weight),
        name="second_layer",
        **cost,
    )
    pieces = exchange(pieces)
    pooled, normed = call(
        coarse_start_kernel,
        (shaped(crows, CWIDTH), shaped(crows, CWIDTH)),
        [],
        (tables, pieces, coarse_gain[None]),
        name="coarse_start",
    )
    up = [(i, (i + 1) % groups) for i in range(groups)]
    down = [(i, (i - 1) % groups) for i in range(groups)]
    half = crows // 2
    left = lax.ppermute(normed, "grp", up)
    right = lax.ppermute(normed, "grp", down)
    own = call(
        project_kernel,
        shaped(crows, 3 * CWIDTH),
        [],
        (normed, coarse_qkv),
        tables=0,
        flops=2 * crows * CWIDTH * 3 * CWIDTH,
        name="own_projection",
    )
    far_a = lax.ppermute(left[:half], "grp", up)
    far_b = lax.ppermute(right[half:], "grp", down)
    wkv = coarse_qkv[:, CWIDTH:]
    left, right = call(
        project_kernel,
        (shaped(crows, 2 * CWIDTH), shaped(crows, 2 * CWIDTH)),
        [],
        (left, right, wkv),
        tables=0,
        flops=8 * crows * CWIDTH * CWIDTH,
        name="near_projection",
    )
    coarse, pieces = call(
        functools.partial(coarse_kernel, groups=groups),
        (shaped(crows, CWIDTH), shaped(SUBS, POOL, CWIDTH)),
        [pltpu.VMEM((groups * crows, 2 * CWIDTH), BF16), pltpu.VMEM((crows, CWIDTH), BF16)],
        (tables, members, lengths, pooled, own, left, right, far_a, far_b, wkv, coarse_out),
        tables=3,
        flops=4 * 10**9,
        exps=2 * 10**6,
        name="coarse_layer",
    )
    pieces = exchange(pieces)
    sent = call(
        third_kernel,
        shaped(SUBS, SUB, width),
        [turn, wide],
        (tables, second, pieces, gains[2], fine_qkv[2], fine_out[2], unpool_weight),
        name="third_layer",
        **cost,
    )
    refined = call(
        ordered_kernel,
        shaped(SUBS, SUB, width),
        [],
        (tables, exchange(sent)),
        name="ordered",
    )
    return refined.reshape(rows, width), coarse


def solution(mesh):
    return jax.shard_map(
        body,
        mesh=mesh,
        in_specs=(
            P(("pts", "grp"), None),
            P(),
            P("pts", None),
            P("pts", None),
            P(),
            P(),
            P(),
            P(),
            P(),
            P(),
            P(),
            P(),
        ),
        out_specs=(P(("pts", "grp"), None), P(("pts", "grp"), None)),
        check_vma=False,
    )
```

profile of v0, /device:TPU:1, one launch (start us, length us, event | category | flops | bytes accessed | tf_op | source)
XLA Modules:
  0.0 187.1 jit_solution(213655567151123493)
XLA Ops:
  0.6 0.8 reshape.53
  1.5 0.8 fusion.1
  2.2 0.1 pad.2.clone
  2.3 1.4 fusion.2
  3.7 0.7 select_reduce_fusion
  4.4 1.8 slice_bitcast_fusion.3
  6.2 2.3 %slice_bitcast_fusion = (bf16[256,768]{1,0:T(8,128)(2,1)}, bf16[256,768]{1,0:T(8,128)(2,1)}, bf16[256,768]{1,0:T(8,128)(2,1)}) fusion(bf16[3,256,768]{2,1,0:T(8,128)(2,1)} %param.17), kind=kLoop, calls=%fused_computation.2 | loop fusion | bytes 2359296 | tf_op jit(solution)/shard_map/squeeze | solution.py:359
  8.5 0.6 add_add_fusion.tables
  9.1 15.4 %first_layer.1 = bf16[32,64,256]{2,1,0:T(8,128)(2,1)} custom-call(s32[3,32]{1,0:T(4,128)} %add_add_fusion.tables, bf16[32,64,256]{2,1,0:T(8,128)(2,1)} %bitcast.36, f32[1,256]{1,0:T(1,128)} %get-tuple-element.27.gain_ref, bf16[256,768]{1,0:T(8,128)(2,1)} %get-tuple-element.21.wqkv_ref, bf16[256,256]{1,0:T(8,128)(2,1)} %get-tuple-element.24.wo_ref), custom_call_target="tpu_custom_call" | custom-call | flops 5000000000 | bytes 3148544 | tf_op jit(solution)/shard_map/first_layer/pallas_call | solution.py:218
  24.5 26.6 %all_to_all.20.x_ref = bf16[32,64,256]{2,1,0:T(8,128)(2,1)} all-to-all(bf16[32,64,256]{2,1,0:T(8,128)(2,1)} %first_layer.1), channel_id=1, replica_groups=mesh['pts'=32,'grp'=4] {'pts'}, dimensions={0} | all-to-all | bytes 2097152 | tf_op jit(solution)/shard_map/all_to_all | solution.py:234
  51.1 0.0 copy-start.5
  51.1 17.7 %second_layer.1 = (bf16[8,256,256]{2,1,0:T(8,128)(2,1)}, bf16[32,16,512]{2,1,0:T(8,128)(2,1)}) custom-call(s32[3,32]{1,0:T(4,128)} %add_add_fusion.tables, bf16[32,64,256]{2,1,0:T(8,128)(2,1)} %all_to_all.20.x_ref, f32[1,256]{1,0:T(1,128)} %get-tuple-element.28.gain_ref, bf16[256,768]{1,0:T(8,128)(2,1)} %get-tuple-element.22.wqkv_ref, ...), custom_call_target="tpu_custom_call" | custom-call | flops 5000000000 | bytes 5245696 | tf_op jit(solution)/shard_map/second_layer/pallas_call | solution.py:218
  68.8 0.0 copy-start
  68.8 4.1 %all-to-all-start.1 = ((bf16[32,16,512]{2,1,0:T(8,128)(2,1)}), bf16[32,16,512]{2,1,0:T(8,128)(2,1)S(1)}, u32[]{:S(2)}, u32[]{:S(2)}) async-start(bf16[32,16,512]{2,1,0:T(8,128)(2,1)} %get-tuple-element.11), calls=%async_computation.1 | async-start | bytes 1048576 | tf_op jit(solution)/shard_map/all_to_all | solution.py:234
  72.9 0.0 copy-done.5
  72.9 0.1 select_reduce_fusion.5
  73.0 0.0 copy-done.4
  73.0 0.2 select_reduce_fusion.4
  73.2 11.2 %all-to-all-done.1.pieces_ref = bf16[32,16,512]{2,1,0:T(8,128)(2,1)S(1)} async-done(((bf16[32,16,512]{2,1,0:T(8,128)(2,1)}), bf16[32,16,512]{2,1,0:T(8,128)(2,1)S(1)}, u32[]{:S(2)}, u32[]{:S(2)}) %all-to-all-start.1) | async-done | bytes 524320 | tf_op jit(solution)/shard_map/all_to_all | solution.py:234
  84.4 0.0 copy-start.1
  84.4 0.8 copy-done.1
  85.2 2.2 %coarse_start.1 = (bf16[512,512]{1,0:T(8,128)(2,1)}, bf16[512,512]{1,0:T(8,128)(2,1)}) custom-call(s32[3,32]{1,0:T(4,128)} %add_add_fusion.tables, bf16[32,16,512]{2,1,0:T(8,128)(2,1)} %copy-done.1, f32[1,512]{1,0:T(1,128)} %bitcast.30), custom_call_target="tpu_custom_call" | custom-call | bytes 1053440 | tf_op jit(solution)/shard_map/coarse_start/pallas_call | solution.py:218
  87.4 2.7 %collective-permute-start.1 = (bf16[512,512]{1,0:T(8,128)(2,1)}, bf16[512,512]{1,0:T(8,128)(2,1)S(1)}, u32[]{:S(2)}, u32[]{:S(2)}) collective-permute-start(bf16[512,512]{1,0:T(8,128)(2,1)} %get-tuple-element.13.refs_0_), channel_id=1, source_target_pairs={{0,3},{1,0},{2,1},{3,2},{4,7},{5,4},{6,5},{7,6},{8,11},{9,8},{10,9... | collective-permute-start | bytes 1572872 | tf_op jit(solution)/shard_map/ppermute | solution.py:322
  90.1 0.0 collective-permute-start
  90.1 0.8 select_reduce_fusion.2
  90.9 0.1 add_minimum_fusion
  90.9 10.4 %collective-permute-done.1.refs_1_ = bf16[512,512]{1,0:T(8,128)(2,1)S(1)} collective-permute-done((bf16[512,512]{1,0:T(8,128)(2,1)}, bf16[512,512]{1,0:T(8,128)(2,1)S(1)}, u32[]{:S(2)}, u32[]{:S(2)}) %collective-permute-start.1) | collective-permute-done | bytes 524320 | tf_op jit(solution)/shard_map/ppermute | solution.py:322
  101.3 0.0 copy-start.2
  101.3 3.4 %collective-permute-start.3 = (bf16[256,512]{1,0:T(8,128)(2,1)S(1)}, bf16[256,512]{1,0:T(8,128)(2,1)S(1)}, u32[]{:S(2)}, u32[]{:S(2)}) collective-permute-start(bf16[256,512]{1,0:T(8,128)(2,1)S(1)} %slice.49), channel_id=1, source_target_pairs={{0,3},{1,0},{2,1},{3,2},{4,7},{5,4},{6,5},{7,6},{8,11},{9,8},{10,9... | collective-permute-start | bytes 786440 | tf_op jit(solution)/shard_map/ppermute | solution.py:333
  104.7 0.0 collective-permute-done.refs_0_
  104.7 0.0 copy-start.3
  104.7 0.1 collective-permute-start.2
  104.8 0.3 select_reduce_fusion.1
  105.1 0.6 reshape.55.blocks
  105.7 0.0 copy-done
  105.7 1.1 slice.42.refs_2_.wkv_ref
  106.8 0.0 copy-done.2
  106.8 3.7 %own_projection.1.own_ref = bf16[512,1536]{1,0:T(8,128)(2,1)} custom-call(bf16[512,512]{1,0:T(8,128)(2,1)} %get-tuple-element.13.refs_0_, bf16[512,1536]{1,0:T(8,128)(2,1)} %refs_1_.1), custom_call_target="tpu_custom_call" | custom-call | flops 805306368 | bytes 4194304 | tf_op jit(solution)/shard_map/own_projection/pallas_call | solution.py:218
  110.6 0.0 copy-done.3
  110.6 3.8 %near_projection.1 = (bf16[512,1024]{1,0:T(8,128)(2,1)}, bf16[512,1024]{1,0:T(8,128)(2,1)}) custom-call(bf16[512,512]{1,0:T(8,128)(2,1)} %copy-done.3, bf16[512,512]{1,0:T(8,128)(2,1)} %copy-done.2, bf16[512,1024]{1,0:T(8,128)(2,1)} %slice.42.refs_2_.wkv_ref), custom_call_target="tpu_custom_call" | custom-call | flops 1073741824 | bytes 4194304 | tf_op jit(solution)/shard_map/near_projection/pallas_call | solution.py:218
  114.4 0.0 collective-permute-done.3.far_b_ref
  114.4 0.0 collective-permute-done.2.far_a_ref
  114.4 0.7 copy-done.6
  115.1 12.3 %coarse_layer.1 = (bf16[512,512]{1,0:T(8,128)(2,1)}, bf16[32,16,512]{2,1,0:T(8,128)(2,1)}) custom-call(s32[3,32]{1,0:T(4,128)} %add_add_fusion.tables, s32[64]{0:T(128)} %reshape.55.blocks, s32[8]{0:T(128)} %get-tuple-element.18.counts, bf16[512,512]{1,0:T(8,128)(2,1)} %get-tuple-element.12.pooled_ref, bf16[512,1536]{1,0:T(8,128)(2,1)} %own_projection.1.own_ref, ...), custom_call_target="tpu_custom_call" | custom-call | flops 4000000000 | bytes 12584256 | tf_op jit(solution)/shard_map/coarse_layer/pallas_call | solution.py:218
  127.4 17.3 %all_to_all.21.coarse_ref = bf16[32,16,512]{2,1,0:T(8,128)(2,1)} all-to-all(bf16[32,16,512]{2,1,0:T(8,128)(2,1)} %get-tuple-element.16), channel_id=1, replica_groups=mesh['pts'=32,'grp'=4] {'pts'}, dimensions={0} | all-to-all | bytes 1048576 | tf_op jit(solution)/shard_map/all_to_all | solution.py:234
  144.7 18.3 %third_layer.1 = bf16[32,64,256]{2,1,0:T(8,128)(2,1)} custom-call(s32[3,32]{1,0:T(4,128)} %add_add_fusion.tables, bf16[8,256,256]{2,1,0:T(8,128)(2,1)} %get-tuple-element.10.x_ref, bf16[32,16,512]{2,1,0:T(8,128)(2,1)} %all_to_all.21.coarse_ref, f32[1,256]{1,0:T(1,128)} %get-tuple-element.26.gain_ref, bf16[256,768]{1,0:T(8,128)(2,1)} %get-tuple-element.20.wqkv_ref, ...), custom_call_target="tpu_custom_call" | custom-call | flops 5000000000 | bytes 6294272 | tf_op jit(solution)/shard_map/third_layer/pallas_call | solution.py:218
  162.9 21.8 %all_to_all.22.x_ref = bf16[32,64,256]{2,1,0:T(8,128)(2,1)} all-to-all(bf16[32,64,256]{2,1,0:T(8,128)(2,1)} %third_layer.1), channel_id=1, replica_groups=mesh['pts'=32,'grp'=4] {'pts'}, dimensions={0} | all-to-all | bytes 2097152 | tf_op jit(solution)/shard_map/all_to_all | solution.py:234
  184.8 2.3 %ordered.1 = bf16[32,64,256]{2,1,0:T(8,128)(2,1)} custom-call(s32[3,32]{1,0:T(4,128)} %add_add_fusion.tables, bf16[32,64,256]{2,1,0:T(8,128)(2,1)} %all_to_all.22.x_ref), custom_call_target="tpu_custom_call" | custom-call | bytes 2097920 | tf_op jit(solution)/shard_map/ordered/pallas_call | solution.py:218
  (7 shorter events, 0.1 us)
Async XLA Ops:
  51.1 21.8 %copy-start.5 = (s32[1,8]{1,0:T(1,128)S(1)}, s32[1,8]{1,0:T(1,128)}, u32[]{:S(2)}) copy-start(s32[1,8]{1,0:T(1,128)} %param.15) | copy-start | bytes 100
  51.1 21.9 %copy-start.4 = (s32[1,32]{1,0:T(1,128)S(1)}, s32[1,32]{1,0:T(1,128)}, u32[]{:S(2)}) copy-start(s32[1,32]{1,0:T(1,128)} %param.14) | copy-start | bytes 388
  68.8 36.9 %copy-start = (bf16[512,1536]{1,0:T(8,128)(2,1)S(1)}, bf16[512,1536]{1,0:T(8,128)(2,1)}, u32[]{:S(2)}) copy-start(bf16[512,1536]{1,0:T(8,128)(2,1)} %refs_1_.1) | copy-start | bytes 4718596
  68.8 15.6 %all-to-all-start.1 = ((bf16[32,16,512]{2,1,0:T(8,128)(2,1)}), bf16[32,16,512]{2,1,0:T(8,128)(2,1)S(1)}, u32[]{:S(2)}, u32[]{:S(2)}) async-start(bf16[32,16,512]{2,1,0:T(8,128)(2,1)} %get-tuple-element.11), calls=%async_computation.1 | async-start | bytes 1048576 | tf_op jit(solution)/shard_map/all_to_all | solution.py:234
  84.4 0.8 copy-start.1
  87.4 13.9 %collective-permute-start.1 = (bf16[512,512]{1,0:T(8,128)(2,1)}, bf16[512,512]{1,0:T(8,128)(2,1)S(1)}, u32[]{:S(2)}, u32[]{:S(2)}) collective-permute-start(bf16[512,512]{1,0:T(8,128)(2,1)} %get-tuple-element.13.refs_0_), channel_id=1, source_target_pairs={{0,3},{1,0},{2,1},{3,2},{4,7},{5,4},{6,5},{7,6},{8,11},{9,8},{10,9... | collective-permute-start | bytes 1572872 | tf_op jit(solution)/shard_map/ppermute | solution.py:322
  90.1 14.6 %collective-permute-start = (bf16[512,512]{1,0:T(8,128)(2,1)}, bf16[512,512]{1,0:T(8,128)(2,1)S(1)}, u32[]{:S(2)}, u32[]{:S(2)}) collective-permute-start(bf16[512,512]{1,0:T(8,128)(2,1)} %get-tuple-element.13.refs_0_), channel_id=1, source_target_pairs={{0,1},{1,2},{2,3},{3,0},{4,5},{5,6},{6,7},{7,4},{8,9},{9,10},{10,1... | collective-permute-start | bytes 1572872 | tf_op jit(solution)/shard_map/ppermute | solution.py:321
  101.3 5.5 %copy-start.2 = (bf16[512,512]{1,0:T(8,128)(2,1)}, bf16[512,512]{1,0:T(8,128)(2,1)S(1)}, u32[]{:S(2)}) copy-start(bf16[512,512]{1,0:T(8,128)(2,1)S(1)} %collective-permute-done.1.refs_1_) | copy-start | bytes 1572868
  101.3 13.0 %collective-permute-start.3 = (bf16[256,512]{1,0:T(8,128)(2,1)S(1)}, bf16[256,512]{1,0:T(8,128)(2,1)S(1)}, u32[]{:S(2)}, u32[]{:S(2)}) collective-permute-start(bf16[256,512]{1,0:T(8,128)(2,1)S(1)} %slice.49), channel_id=1, source_target_pairs={{0,3},{1,0},{2,1},{3,2},{4,7},{5,4},{6,5},{7,6},{8,11},{9,8},{10,9... | collective-permute-start | bytes 786440 | tf_op jit(solution)/shard_map/ppermute | solution.py:333
  104.7 5.9 %copy-start.3 = (bf16[512,512]{1,0:T(8,128)(2,1)}, bf16[512,512]{1,0:T(8,128)(2,1)S(1)}, u32[]{:S(2)}) copy-start(bf16[512,512]{1,0:T(8,128)(2,1)S(1)} %collective-permute-done.refs_0_) | copy-start | bytes 1572868
  104.7 9.6 %collective-permute-start.2 = (bf16[256,512]{1,0:T(8,128)(2,1)S(1)}, bf16[256,512]{1,0:T(8,128)(2,1)}, u32[]{:S(2)}, u32[]{:S(2)}) collective-permute-start(bf16[256,512]{1,0:T(8,128)(2,1)S(1)} %slice.48), channel_id=1, source_target_pairs={{0,1},{1,2},{2,3},{3,0},{4,5},{5,6},{6,7},{7,4},{8,9},{9,10},{10,1... | collective-permute-start | bytes 786440 | tf_op jit(solution)/shard_map/ppermute | solution.py:332
  114.4 0.7 copy-start.6
where the time goes:
time: 188 us; the launch traced here: 187 us
  Pallas kernels  75.6 us (40%)
  blocking collectives  65.7 us (35%)
  waiting for transfers between devices  21.6 us (11%)
  starting transfers between devices  10.3 us (5%)
  local copies, waits for them, and re-layouts  9.62 us (5%)
  other arithmetic  3.52 us (2%)
    pallas_call x8, Pallas kernels, call(): pl.pallas_call(kernel, out_shape=outs, in_specs=[SMEM] * tables + [VMEM]...  75.6 us
    all_to_all x3, blocking collectives, exchange(): lax.all_to_all(pieces, 'pts', split_axis=0, concat_axis=0, tiled=True)  65.7 us
    all_to_all x1, waiting for transfers between devices, exchange(): lax.all_to_all(pieces, 'pts', split_axis=0, concat_axis=0, tiled=True)  11.2 us
    ppermute x1, waiting for transfers between devices, body(): right = lax.ppermute(normed, 'grp', down)  10.4 us
    all_to_all x1, starting transfers between devices, exchange(): lax.all_to_all(pieces, 'pts', split_axis=0, concat_axis=0, tiled=True)  4.07 us
  transfers between devices with their start and end apart: 5, of which 2 were waited for; matrix products, arithmetic and copies ran while one was open for 2% of the time, Pallas kernels for 4%

commit v1 on v0

v1 whole, which is shorter than its diff:
```python
import functools
import math

import jax
import jax.numpy as jnp
from jax import lax
from jax.experimental import pallas as pl
from jax.experimental.pallas import tpu as pltpu
from jax.sharding import PartitionSpec as P

F32, BF16 = jnp.float32, jnp.bfloat16
HEADS = 8
BALL = 256
SUB = 64
CBLK = 64
MOST_BALL = 8
WIDTH = 256
CWIDTH = 512
SUBS = 32
POOL = 16
LOG2E = 1.4426950408889634
NT = (((1,), (1,)), ((), ()))
TN = (((0,), (0,)), ((), ()))
VMEM = pl.BlockSpec(memory_space=pltpu.VMEM)
SMEM = pl.BlockSpec(memory_space=pltpu.SMEM)


def dot(a, b, dims=None):
    if dims is None:
        return jnp.dot(a, b, preferred_element_type=F32)
    return lax.dot_general(a, b, dims, preferred_element_type=F32)


def norm(x, gain):
    return (x * lax.rsqrt(jnp.mean(x * x, axis=-1, keepdims=True) + 1e-6) * gain).astype(BF16)


def head_masks():
    lane = lax.broadcasted_iota(jnp.int32, (1, 128), 1) // 32
    return [(lane == i).astype(F32).astype(BF16) for i in range(4)]


SCALE = LOG2E / math.sqrt(32.0)
BALLS = SUBS // 4
VM = pltpu.VMEM


def transposed(wqkv_ref, wqvt_ref):
    wqvt_ref[:WIDTH] = wqkv_ref[:, :WIDTH].T
    wqvt_ref[WIDTH:] = wqkv_ref[:, 2 * WIDTH :].T


def fine_layer(load, reload, store, gain, wqvt_ref, wk_ref, wo_ref, scores, bufs, ready=None):
    left, right = scores
    k_s, qt_s, vt_s, ot_s = bufs[0:2], bufs[2:4], bufs[4:6], bufs[6:8]
    masks = head_masks()
    ones = jnp.ones((16, BALL), BF16)

    def project(b, par):
        h = norm(load(b), gain)
        qv = dot(wqvt_ref[...], h, NT)
        qt_s[par][...] = (qv[:WIDTH] * SCALE).astype(BF16)
        vt_s[par][...] = qv[WIDTH:].astype(BF16)
        k_s[par][...] = dot(h, wk_ref[...]).astype(BF16)

    def score(dst, par, g, i):
        keys = k_s[par][:, 128 * g : 128 * g + 128] * masks[i]
        dst[BALL * i : BALL * (i + 1)] = dot(keys, qt_s[par][128 * g : 128 * g + 128, :])

    def soft(src, par, g, i):
        s = src[BALL * i : BALL * (i + 1)]
        p = jnp.exp2(s - jnp.max(s, axis=0, keepdims=True)).astype(BF16)
        at = 32 * (4 * g + i)
        o = dot(jnp.concatenate([vt_s[par][at : at + 32], ones], axis=0), p)
        ot_s[par][at : at + 32] = (o[:32] * (1.0 / o[32:33])).astype(BF16)

    def finish(b, par):
        store(b, (reload(b) + dot(ot_s[par][...], wo_ref[...], TN)).astype(BF16))

    ot_s[1][...] = jnp.zeros_like(ot_s[1])
    project(0, 0)
    for i in range(4):
        score(left, 0, 0, i)
    if ready is not None:
        ready()

    def step(b, par):
        project(jnp.minimum(b + 1, BALLS - 1), 1 - par)
        for i in range(4):
            score(right, par, 1, i)
            soft(left, par, 0, i)
        finish(jnp.maximum(b - 1, 0), 1 - par)
        for i in range(4):
            score(left, 1 - par, 0, i)
            soft(right, par, 1, i)

    def pair(t, carry):
        step(2 * t, 0)
        step(2 * t + 1, 1)
        return carry

    lax.fori_loop(0, BALLS // 2, pair, 0)
    finish(BALLS - 1, 1)


FINE_SCRATCH = [VM((4 * BALL, BALL), F32)] * 2 + [VM((BALL, WIDTH), BF16)] * 8


def first_kernel(
    rot, gain_ref, x_hbm, wqkv_hbm, wo_hbm, out_ref, wqvt_ref, x_ref, wqkv_ref, wo_ref, sems, *scratch
):
    groups = lax.axis_size("grp")
    device = lax.axis_index("pts") * groups + lax.axis_index("grp")
    copies = [
        pltpu.make_async_copy(wqkv_hbm.at[0], wqkv_ref, sems.at[0]),
        pltpu.make_async_copy(x_hbm.at[pl.ds(0, 4)], x_ref.at[pl.ds(0, 4)], sems.at[1]),
        pltpu.make_async_copy(wo_hbm.at[0], wo_ref, sems.at[2]),
        pltpu.make_async_copy(x_hbm.at[pl.ds(4, SUBS - 4)], x_ref.at[pl.ds(4, SUBS - 4)], sems.at[3]),
    ]
    for copy in copies:
        copy.start()
    copies[0].wait()
    transposed(wqkv_ref, wqvt_ref)
    copies[1].wait()

    def ready():
        copies[2].wait()
        copies[3].wait()

    def load(b):
        return x_ref[pl.ds(4 * b, 4)].reshape(BALL, WIDTH).astype(F32)

    def store(b, y):
        for i in range(4):
            out_ref[rot[device * SUBS + 4 * b + i] // (SUBS * groups)] = y[SUB * i : SUB * (i + 1)]

    wk_ref = wqkv_ref.at[:, WIDTH : 2 * WIDTH]
    fine_layer(
        load, load, store, gain_ref[...], wqvt_ref, wk_ref, wo_ref, scratch[:2], scratch[2:], ready
    )


def second_kernel(
    place, x_ref, gain_ref, wqvt_ref, wk_ref, wo_ref, pool_ref, out_ref, pooled_ref, wide_ref, *scratch
):
    def load(b):
        return jnp.concatenate([x_ref[place[4 * b + i]] for i in range(4)], axis=0).astype(F32)

    def store(b, y):
        out_ref[b] = y
        wide = y.astype(F32)
        for c in range(2):
            wide_ref[c] = wide[:, 128 * c : 128 * c + 128]
        rows = jnp.concatenate(
            [wide_ref[c, pl.ds(j, BALL // 4, stride=4)] for j in range(4) for c in range(2)],
            axis=1,
        ).astype(BF16)
        pooled = dot(rows, pool_ref[...]).astype(BF16)
        for i in range(4):
            pooled_ref[place[4 * b + i]] = pooled[POOL * i : POOL * (i + 1)]

    fine_layer(load, load, store, gain_ref[...], wqvt_ref, wk_ref, wo_ref, scratch[:2], scratch[2:])


def third_kernel(
    place, x_ref, coarse_ref, gain_ref, wqvt_ref, wk_ref, wo_ref, unpool_ref, out_ref,
    wide_ref, held_ref, *scratch
):
    def load(b):
        coarse = jnp.concatenate([coarse_ref[place[4 * b + i]] for i in range(4)], axis=0)
        lifted = dot(coarse, unpool_ref[...])
        for j in range(4):
            for c in range(2):
                at = WIDTH * j + 128 * c
                wide_ref[c, pl.ds(j, BALL // 4, stride=4)] = lifted[:, at : at + 128]
        x = x_ref[b].astype(F32) + jnp.concatenate([wide_ref[0], wide_ref[1]], axis=1)
        held_ref[b] = x.astype(BF16)
        return x.astype(BF16).astype(F32)

    def reload(b):
        return held_ref[b].astype(F32)

    def store(b, y):
        for i in range(4):
            out_ref[place[4 * b + i]] = y[SUB * i : SUB * (i + 1)]

    fine_layer(load, reload, store, gain_ref[...], wqvt_ref, wk_ref, wo_ref, scratch[:2], scratch[2:])


def group_of(step):
    return lax.rem(lax.axis_index("grp") + step, lax.axis_size("grp"))


def tree_rows(pieces, table, group):
    return jnp.concatenate([pieces(table[group, s]) for s in range(SUBS)], axis=0)


def own_kernel(table, pieces_ref, gain_ref, w_ref, pooled_ref, out_ref):
    pooled_ref[...] = tree_rows(lambda k: pieces_ref[k], table, group_of(0))
    out_ref[...] = dot(norm(pooled_ref[...].astype(F32), gain_ref[...]), w_ref[...]).astype(BF16)


def near_kernel(table, la_ref, lb_ref, ra_ref, rb_ref, gain_ref, w_ref, left_ref, right_ref, all_ref):
    groups = lax.axis_size("grp")
    half = SUBS // 2
    for step, a_ref, b_ref, out_ref in ((groups - 1, la_ref, lb_ref, left_ref), (1, ra_ref, rb_ref, right_ref)):
        all_ref[:half] = a_ref[...]
        all_ref[half:] = b_ref[...]
        rows = tree_rows(lambda k: all_ref[k], table, group_of(step)).astype(F32)
        out_ref[...] = dot(norm(rows, gain_ref[...]), w_ref[:, CWIDTH:]).astype(BF16)


def coarse_kernel(
    table, blocks, counts, pooled_ref, own_ref, left_ref, right_ref, far_a_ref, far_b_ref,
    gain_ref, w_ref, wo_ref, coarse_ref, sent_ref, kv_ref, all_ref, att_ref, a_ref, b_ref,
):
    groups = lax.axis_size("grp")
    me = lax.axis_index("grp")
    rows = CWIDTH
    half = SUBS // 2
    all_ref[:half] = far_a_ref[...]
    all_ref[half:] = far_b_ref[...]
    far = norm(tree_rows(lambda k: all_ref[k], table, group_of(2)).astype(F32), gain_ref[...])
    at = pl.multiple_of(group_of(2) * rows, rows)
    kv_ref[pl.ds(at, rows)] = dot(far, w_ref[:, CWIDTH:]).astype(BF16)
    for step, ref in ((0, own_ref), (groups - 1, left_ref), (1, right_ref)):
        at = pl.multiple_of(group_of(step) * rows, rows)
        kv_ref[pl.ds(at, rows)] = ref[:, ref.shape[1] - 2 * CWIDTH :]
    size = 64
    lanes = lax.broadcasted_iota(jnp.int32, (1, 256), 1) // size
    keep = [(lanes == i).astype(F32) for i in range(4)]
    keep_low = [m.astype(BF16) for m in keep]
    member = lax.broadcasted_iota(jnp.int32, (1, MOST_BALL * CBLK), 1) // CBLK

    def members(b, at):
        starts = [pl.multiple_of(blocks[b * MOST_BALL + m] * CBLK, CBLK) for m in range(MOST_BALL)]
        return jnp.concatenate([kv_ref[pl.ds(s, CBLK), at : at + 256] for s in starts], axis=0)

    def score(dst, b, g):
        q = own_ref[pl.ds(pl.multiple_of(b * CBLK, CBLK), CBLK), 256 * g : 256 * g + 256]
        spread = jnp.concatenate([q * keep_low[i] for i in range(4)], axis=0)
        scores = dot(spread, members(b, 256 * g), NT) * (LOG2E / 8.0)
        dst[...] = jnp.where(member < counts[b], scores, -jnp.inf)

    def soft(src, b, g):
        scores = src[...]
        expo = jnp.exp2(scores - jnp.max(scores, axis=-1, keepdims=True))
        scale = 1.0 / jnp.sum(expo, axis=-1, keepdims=True)
        out = dot(expo.astype(BF16), members(b, CWIDTH + 256 * g)) * scale
        total = sum(out[CBLK * i : CBLK * (i + 1)] * keep[i] for i in range(4))
        begin = pl.multiple_of(b * CBLK, CBLK)
        att_ref[pl.ds(begin, CBLK), 256 * g : 256 * g + 256] = total.astype(BF16)

    count = rows // CBLK
    score(a_ref, 0, 0)

    def block(b, carry):
        score(b_ref, b, 1)
        soft(a_ref, b, 0)
        score(a_ref, jnp.minimum(b + 1, count - 1), 0)
        soft(b_ref, b, 1)
        return carry

    lax.fori_loop(0, count, block, 0)
    result = (pooled_ref[...].astype(F32) + dot(att_ref[...], wo_ref[...])).astype(BF16)
    coarse_ref[...] = result
    for s in range(SUBS):
        sent_ref[table[me, s]] = result[POOL * s : POOL * (s + 1)]


def call(kernel, outs, scratch, args, tables=1, flops=0, exps=0, name=None, grant=16, specs=None):
    size = sum(a.size * a.dtype.itemsize for a in args)
    return pl.pallas_call(
        kernel,
        out_shape=outs,
        in_specs=specs or [SMEM] * tables + [VMEM] * (len(args) - tables),
        out_specs=jax.tree.map(lambda _: VMEM, outs),
        scratch_shapes=scratch,
        name=name,
        compiler_params=pltpu.CompilerParams(vmem_limit_bytes=grant << 20),
        cost_estimate=pl.CostEstimate(flops=flops, bytes_accessed=2 * size, transcendentals=exps),
    )(*args)


def shaped(*shape):
    return jax.ShapeDtypeStruct(shape, BF16)


def exchange(pieces):
    return lax.all_to_all(pieces, "pts", split_axis=0, concat_axis=0, tiled=True)


def tables_of(rot_dest):
    points, groups = lax.axis_size("pts"), lax.axis_size("grp")
    point, group = lax.axis_index("pts"), lax.axis_index("grp")
    device = point * groups + group
    local = lax.dynamic_slice_in_dim(rot_dest, point * groups * SUBS, groups * SUBS)
    targets = (local // SUBS // groups).reshape(groups, SUBS)
    mine = lax.dynamic_index_in_dim(rot_dest.reshape(points, groups, SUBS), group, 1, False)
    slot = mine - device * SUBS
    source = jnp.arange(points, dtype=jnp.int32)
    hit = slot[None] == jnp.arange(SUBS, dtype=jnp.int32)[:, None, None]
    place = jnp.sum(jnp.where(hit, source[None, :, None], 0), axis=(1, 2))
    return targets, place.astype(jnp.int32)


def ball_table(order, sizes, count):
    total = order.shape[0]
    before = jnp.arange(sizes.shape[0])
    ends = jnp.sum(jnp.where(before[None, :] <= before[:, None], sizes[None, :], 0), axis=1)
    starts = ends - sizes
    marks = jnp.arange(total, dtype=jnp.int32)
    mine = lax.axis_index("grp") * count + jnp.arange(count, dtype=jnp.int32)
    where = jnp.sum(jnp.where(order[None, :] == mine[:, None], marks[None, :], 0), axis=1)
    inside = (starts[None, :] <= where[:, None]) & (where[:, None] < ends[None, :])
    first = jnp.sum(jnp.where(inside, starts[None, :], 0), axis=1)
    length = jnp.sum(jnp.where(inside, sizes[None, :], 0), axis=1)
    slots = jnp.arange(MOST_BALL, dtype=jnp.int32)
    place = jnp.minimum(first[:, None] + slots[None, :], total - 1)
    members = jnp.sum(
        jnp.where(place[:, :, None] == marks[None, None, :], order[None, None, :], 0), axis=2
    )
    return members.reshape(-1).astype(jnp.int32), length.astype(jnp.int32)


def body(
    points,
    rot_dest,
    block_order,
    ball_sizes,
    fine_gain,
    fine_qkv,
    fine_out,
    pool_weight,
    coarse_gain,
    coarse_qkv,
    coarse_out,
    unpool_weight,
):
    rows, width = points.shape
    groups = lax.axis_size("grp")
    crows = rows // 4
    wide = VM((2, BALL, 128), F32)
    cost = dict(flops=5 * 10**9, exps=4 * 10**6)
    sent = call(
        first_kernel,
        shaped(SUBS, SUB, width),
        [
            VM((2 * width, width), BF16),
            VM((SUBS, SUB, width), BF16),
            VM((width, 3 * width), BF16),
            VM((width, width), BF16),
            pltpu.SemaphoreType.DMA((4,)),
        ]
        + FINE_SCRATCH,
        (rot_dest, fine_gain[0:1], points.reshape(SUBS, SUB, width), fine_qkv, fine_out),
        specs=[SMEM, VMEM] + [pl.BlockSpec(memory_space=pl.ANY)] * 3,
        grant=60,
        name="first_layer",
        **cost,
    )
    sent, rot_dest, block_order, ball_sizes, fine_qkv, fine_out, fine_gain = lax.optimization_barrier(
        (sent, rot_dest, block_order, ball_sizes, fine_qkv, fine_out, fine_gain)
    )
    targets, place = tables_of(rot_dest)
    members, lengths = ball_table(block_order[0], ball_sizes[0], crows // CBLK)
    gains = [fine_gain[j : j + 1] for j in range(3)]
    turned = [
        jnp.concatenate([w[:, :width].T, w[:, 2 * width :].T], axis=0) for w in (fine_qkv[1], fine_qkv[2])
    ]
    keys = [w[:, width : 2 * width] for w in (fine_qkv[1], fine_qkv[2])]

    arrived = exchange(sent)
    second, pieces = call(
        second_kernel,
        (shaped(BALLS, BALL, width), shaped(SUBS, POOL, CWIDTH)),
        [wide] + FINE_SCRATCH,
        (place, arrived, gains[1], turned[0], keys[0], fine_out[1], pool_weight),
        name="second_layer",
        **cost,
    )
    pieces = exchange(pieces)
    up = [(i, (i + 1) % groups) for i in range(groups)]
    down = [(i, (i - 1) % groups) for i in range(groups)]
    half = SUBS // 2
    left_a = lax.ppermute(pieces[:half], "grp", up)
    right_b = lax.ppermute(pieces[half:], "grp", down)
    left_b = lax.ppermute(pieces[half:], "grp", up)
    right_a = lax.ppermute(pieces[:half], "grp", down)
    gain = coarse_gain[None]
    pooled, own = call(
        own_kernel,
        (shaped(crows, CWIDTH), shaped(crows, 3 * CWIDTH)),
        [],
        (targets, pieces, gain, coarse_qkv),
        flops=2 * crows * CWIDTH * 3 * CWIDTH,
        name="own_projection",
    )
    far_a = lax.ppermute(left_a, "grp", up)
    far_b = lax.ppermute(right_b, "grp", down)
    left, right = call(
        near_kernel,
        (shaped(crows, 2 * CWIDTH), shaped(crows, 2 * CWIDTH)),
        [VM((SUBS, POOL, CWIDTH), BF16)],
        (targets, left_a, left_b, right_a, right_b, gain, coarse_qkv),
        flops=8 * crows * CWIDTH * CWIDTH,
        name="near_projection",
    )
    coarse, pieces = call(
        coarse_kernel,
        (shaped(crows, CWIDTH), shaped(SUBS, POOL, CWIDTH)),
        [
            VM((groups * crows, 2 * CWIDTH), BF16),
            VM((SUBS, POOL, CWIDTH), BF16),
            VM((crows, CWIDTH), BF16),
            VM((4 * CBLK, MOST_BALL * CBLK), F32),
            VM((4 * CBLK, MOST_BALL * CBLK), F32),
        ],
        (targets, members, lengths, pooled, own, left, right, far_a, far_b, gain, coarse_qkv, coarse_out),
        tables=3,
        flops=4 * 10**9,
        exps=2 * 10**6,
        name="coarse_layer",
        grant=24,
    )
    pieces = exchange(pieces)
    sent = call(
        third_kernel,
        shaped(SUBS, SUB, width),
        [wide, VM((BALLS, BALL, width), BF16)] + FINE_SCRATCH,
        (place, second, pieces, gains[2], turned[1], keys[1], fine_out[2], unpool_weight),
        name="third_layer",
        **cost,
    )
    mine = lax.dynamic_index_in_dim(targets, lax.axis_index("grp"), 0, False)
    refined = exchange(sent).at[mine].get(mode="promise_in_bounds", unique_indices=True)
    return refined.reshape(rows, width), coarse


def solution(mesh):
    return jax.shard_map(
        body,
        mesh=mesh,
        in_specs=(
            P(("pts", "grp"), None),
            P(),
            P("pts", None),
            P("pts", None),
            P(),
            P(),
            P(),
            P(),
            P(),
            P(),
            P(),
            P(),
        ),
        out_specs=(P(("pts", "grp"), None), P(("pts", "grp"), None)),
        check_vma=False,
    )
```

time: 188 us -> 147 us (0.78)
  blocking collectives: 65.7 us -> 0 us
  waiting for transfers between devices: 21.6 us -> 61.1 us
  Pallas kernels: 75.6 us -> 44.1 us
  starting transfers between devices: 10.3 us -> 30.8 us
    all_to_all x3 -> x0, blocking collectives: 65.7 us -> none  [exchange(): lax.all_to_all(pieces, 'pts', split_axis=0, concat_axis=0, tiled=True)]
    all_to_all x1 -> x4, waiting for transfers between devices: 11.2 us -> 53.7 us  [exchange(): lax.all_to_all(pieces, 'pts', split_axis=0, concat_axis=0, tiled=True)]
    pallas_call x8 -> x6, Pallas kernels: 75.6 us -> 44.1 us  [call(): pl.pallas_call(kernel, out_shape=outs, in_specs=specs or [SMEM] * tables...]
    all_to_all x1 -> x4, starting transfers between devices: 4.07 us -> 22.7 us  [exchange(): lax.all_to_all(pieces, 'pts', split_axis=0, concat_axis=0, tiled=True)]
    ppermute x4 -> x6, waiting for transfers between devices: 10.4 us -> 7.39 us  [the longest x1 3.34 us: body(): left_a = lax.ppermute(pieces[:half], 'grp', up)]
    squeeze x1, local copies, waits for them, and re-layouts: 2.27 us -> 0.05 us  [body(): fine_qkv[2]]
    ppermute x4 -> x6, starting transfers between devices: 6.19 us -> 8.08 us  [the longest x1 2.67 us: body(): far_b = lax.ppermute(right_b, 'grp', down)]
  transfers between devices with their start and end apart: 5 -> 10, of which waited for: 2 -> 7; matrix products, arithmetic and copies ran while one was open for 2% -> 2% of each run, Pallas kernels for 4% -> 3%
where the time goes in v1:
time: 147 us
  waiting for transfers between devices  61.1 us (42%)
  Pallas kernels  44.1 us (30%)
  starting transfers between devices  30.8 us (21%)
  local copies, waits for them, and re-layouts  8.08 us (5%)
  other arithmetic  1.67 us (1%)
    all_to_all x4, waiting for transfers between devices, exchange(): lax.all_to_all(pieces, 'pts', split_axis=0, concat_axis=0, tiled=True)  53.7 us
    pallas_call x6, Pallas kernels, call(): pl.pallas_call(kernel, out_shape=outs, in_specs=specs or [SMEM] * tables...  44.1 us
    all_to_all x4, starting transfers between devices, exchange(): lax.all_to_all(pieces, 'pts', split_axis=0, concat_axis=0, tiled=True)  22.7 us
    ppermute x1, waiting for transfers between devices, body(): left_a = lax.ppermute(pieces[:half], 'grp', up)  3.34 us
    ppermute x1, waiting for transfers between devices, body(): far_a = lax.ppermute(left_a, 'grp', up)  3.04 us
  transfers between devices with their start and end apart: 10, of which 7 were waited for; matrix products, arithmetic and copies ran while one was open for 2% of the time, Pallas kernels for 3%

profile of v1, /device:TPU:1, one launch (start us, length us, event | category | flops | bytes accessed | tf_op | source)
XLA Modules:
  0.0 146.7 jit_solution(739434899441228769)
XLA Ops:
  0.6 1.3 slice.49.gain_ref
  1.9 9.6 %first_layer.1 = bf16[32,64,256]{2,1,0:T(8,128)(2,1)} custom-call(s32[4096]{0:T(1024)} %rot.1, f32[1,256]{1,0:T(1,128)} %slice.49.gain_ref, bf16[32,64,256]{2,1,0:T(8,128)(2,1)} %bitcast.41, bf16[3,256,768]{2,1,0:T(8,128)(2,1)} %wqkv_hbm.1, bf16[3,256,256]{2,1,0:T(8,128)(2,1)} %wo_hbm.1), custom_call_target="tpu_custom_call" | custom-call | flops 5000000000 | bytes 5277696 | tf_op jit(solution)/shard_map/first_layer/pallas_call | solution.py:273
  11.5 0.0 copy-start.7
  11.5 9.6 %all-to-all-start = ((bf16[32,64,256]{2,1,0:T(8,128)(2,1)}), bf16[32,64,256]{2,1,0:T(8,128)(2,1)S(1)}, u32[]{:S(2)}, u32[]{:S(2)}) async-start(bf16[32,64,256]{2,1,0:T(8,128)(2,1)} %first_layer.1), calls=%async_computation | async-start | bytes 2097152 | tf_op jit(solution)/shard_map/all_to_all | solution.py:290
  21.1 0.0 copy-start.8
  21.1 0.0 copy-start.11
  21.1 0.0 copy-start.9
  21.1 0.1 slice_bitcast_fusion
  21.2 0.0 copy-start.1
  21.2 0.6 copy-done.8
  21.8 0.1 reshape.85
  21.9 0.1 copy.18.wqvt_ref
  22.1 0.1 select_reduce_fusion.5
  22.2 0.7 select_reduce_fusion.place
  22.9 1.0 slice_bitcast_fusion.6
  23.9 14.2 %all-to-all-done.x_ref = bf16[32,64,256]{2,1,0:T(8,128)(2,1)S(1)} async-done(((bf16[32,64,256]{2,1,0:T(8,128)(2,1)}), bf16[32,64,256]{2,1,0:T(8,128)(2,1)S(1)}, u32[]{:S(2)}, u32[]{:S(2)}) %all-to-all-start) | async-done | bytes 1048608 | tf_op jit(solution)/shard_map/all_to_all | solution.py:290
  38.1 10.4 %second_layer.1 = (bf16[8,256,256]{2,1,0:T(8,128)(2,1)S(1)}, bf16[32,16,512]{2,1,0:T(8,128)(2,1)}) custom-call(s32[32]{0:T(128)S(1)} %select_reduce_fusion.place, bf16[32,64,256]{2,1,0:T(8,128)(2,1)S(1)} %all-to-all-done.x_ref, f32[1,256]{1,0:T(1,128)S(1)} %get-tuple-element.47.gain_ref, bf16[512,256]{1,0:T(8,128)(2,1)S(1)} %copy.18.wqvt_ref, ...), custom_call_target="tpu_custom_call" | custom-call | flops 5000000000 | bytes 5245184 | tf_op jit(solution)/shard_map/second_layer/pallas_call | solution.py:273
  48.6 1.0 copy-done.5
  49.5 4.1 %all-to-all-start.1 = ((bf16[32,16,512]{2,1,0:T(8,128)(2,1)}), bf16[32,16,512]{2,1,0:T(8,128)(2,1)S(1)}, u32[]{:S(2)}, u32[]{:S(2)}) async-start(bf16[32,16,512]{2,1,0:T(8,128)(2,1)} %get-tuple-element.25), calls=%async_computation.1 | async-start | bytes 1048576 | tf_op jit(solution)/shard_map/all_to_all | solution.py:290
  53.6 0.2 select_reduce_fusion.4
  53.8 0.2 select_reduce_fusion.2
  54.0 11.1 %all-to-all-done.1.pieces_ref = bf16[32,16,512]{2,1,0:T(8,128)(2,1)S(1)} async-done(((bf16[32,16,512]{2,1,0:T(8,128)(2,1)}), bf16[32,16,512]{2,1,0:T(8,128)(2,1)S(1)}, u32[]{:S(2)}, u32[]{:S(2)}) %all-to-all-start.1) | async-done | bytes 524320 | tf_op jit(solution)/shard_map/all_to_all | solution.py:290
  65.2 0.8 fusion.2
  66.0 1.3 collective-permute-start
  67.3 1.4 collective-permute-start.3
  68.7 0.1 add_minimum_fusion
  68.8 0.0 collective-permute-start.1
  68.8 2.6 %collective-permute-start.2 = (bf16[16,16,512]{2,1,0:T(8,128)(2,1)}, bf16[16,16,512]{2,1,0:T(8,128)(2,1)}, u32[]{:S(2)}, u32[]{:S(2)}) collective-permute-start(bf16[16,16,512]{2,1,0:T(8,128)(2,1)} %get-tuple-element.37), channel_id=1, source_target_pairs={{0,3},{1,0},{2,1},{3,2},{4,7},{5,4},{6,5},{7,6},{8,11},{9,8},{10,9... | collective-permute-start | bytes 786440 | tf_op jit(solution)/shard_map/ppermute | solution.py:389
  71.5 0.1 and_select_fusion
  71.5 0.1 reshape.86.table
  71.6 3.3 %collective-permute-done.la_ref = bf16[16,16,512]{2,1,0:T(8,128)(2,1)S(1)} collective-permute-done((bf16[16,16,512]{2,1,0:T(8,128)(2,1)}, bf16[16,16,512]{2,1,0:T(8,128)(2,1)S(1)}, u32[]{:S(2)}, u32[]{:S(2)}) %collective-permute-start) | collective-permute-done | bytes 262176 | tf_op jit(solution)/shard_map/ppermute | solution.py:386
  75.0 2.7 %collective-permute-start.5 = (bf16[16,16,512]{2,1,0:T(8,128)(2,1)S(1)}, bf16[16,16,512]{2,1,0:T(8,128)(2,1)}, u32[]{:S(2)}, u32[]{:S(2)}) collective-permute-start(bf16[16,16,512]{2,1,0:T(8,128)(2,1)S(1)} %collective-permute-done.3.rb_ref), channel_id=1, source_target_pairs={{0,3},{1,0},{2,1},{3,2},{4,7},{5,4},{6,5},{7,6},{8,11},{9,8},{10,9... | collective-permute-start | bytes 786440 | tf_op jit(solution)/shard_map/ppermute | solution.py:400
  77.6 0.3 select_reduce_fusion.1
  77.9 0.1 reshape.87.blocks
  78.0 1.6 %own_projection.1 = (bf16[512,512]{1,0:T(8,128)(2,1)S(1)}, bf16[512,1536]{1,0:T(8,128)(2,1)S(1)}) custom-call(s32[4,32]{1,0:T(4,128)S(1)} %reshape.86.table, bf16[32,16,512]{2,1,0:T(8,128)(2,1)S(1)} %all-to-all-done.1.pieces_ref, f32[1,512]{1,0:T(1,128)S(1)} %bitcast.32, bf16[512,1536]{1,0:T(8,128)(2,1)S(1)} %copy-done), custom_call_target="tpu_custom_call" | custom-call | flops 805306368 | bytes 4199424 | tf_op jit(solution)/shard_map/own_projection/pallas_call | solution.py:273
  79.7 0.0 copy-start.3
  79.7 1.0 collective-permute-done.1.lb_ref
  80.7 2.5 %near_projection.1 = (bf16[512,1024]{1,0:T(8,128)(2,1)S(1)}, bf16[512,1024]{1,0:T(8,128)(2,1)S(1)}) custom-call(s32[4,32]{1,0:T(4,128)S(1)} %reshape.86.table, bf16[16,16,512]{2,1,0:T(8,128)(2,1)S(1)} %collective-permute-done.la_ref, bf16[16,16,512]{2,1,0:T(8,128)(2,1)} %collective-permute-done.1.lb_ref, bf16[16,16,512]{2,1,0:T(8,128)(2,1)} %collective-permute-done.2.ra_ref, ...), custom_call_target="tpu_custom_call" | custom-call | flops 1073741824 | bytes 5248000 | tf_op jit(solution)/shard_map/near_projection/pallas_call | solution.py:273
  83.2 3.0 %collective-permute-done.4.far_a_ref = bf16[16,16,512]{2,1,0:T(8,128)(2,1)S(1)} collective-permute-done((bf16[16,16,512]{2,1,0:T(8,128)(2,1)S(1)}, bf16[16,16,512]{2,1,0:T(8,128)(2,1)S(1)}, u32[]{:S(2)}, u32[]{:S(2)}) %collective-permute-start.4) | collective-permute-done | bytes 262176 | tf_op jit(solution)/shard_map/ppermute | solution.py:399
  86.2 8.8 %coarse_layer.1 = (bf16[512,512]{1,0:T(8,128)(2,1)}, bf16[32,16,512]{2,1,0:T(8,128)(2,1)}) custom-call(s32[4,32]{1,0:T(4,128)S(1)} %reshape.86.table, s32[64]{0:T(128)S(1)} %reshape.87.blocks, s32[8]{0:T(128)S(1)} %get-tuple-element.32.counts, bf16[512,512]{1,0:T(8,128)(2,1)S(1)} %get-tuple-element.26.pooled_ref, ...), custom_call_target="tpu_custom_call" | custom-call | flops 4000000000 | bytes 13637184 | tf_op jit(solution)/shard_map/coarse_layer/pallas_call | solution.py:273
  95.0 5.1 %all-to-all-start.2 = ((bf16[32,16,512]{2,1,0:T(8,128)(2,1)}), bf16[32,16,512]{2,1,0:T(8,128)(2,1)S(1)}, u32[]{:S(2)}, u32[]{:S(2)}) async-start(bf16[32,16,512]{2,1,0:T(8,128)(2,1)} %get-tuple-element.30), calls=%async_computation.2 | async-start | bytes 1048576 | tf_op jit(solution)/shard_map/all_to_all | solution.py:290
  100.2 0.1 copy.19.wqvt_ref
  100.3 11.2 %all-to-all-done.2.coarse_ref = bf16[32,16,512]{2,1,0:T(8,128)(2,1)S(1)} async-done(((bf16[32,16,512]{2,1,0:T(8,128)(2,1)}), bf16[32,16,512]{2,1,0:T(8,128)(2,1)S(1)}, u32[]{:S(2)}, u32[]{:S(2)}) %all-to-all-start.2) | async-done | bytes 524320 | tf_op jit(solution)/shard_map/all_to_all | solution.py:290
  111.6 1.2 copy-done.6
  112.8 11.2 %third_layer.1 = bf16[32,64,256]{2,1,0:T(8,128)(2,1)} custom-call(s32[32]{0:T(128)S(1)} %select_reduce_fusion.place, bf16[8,256,256]{2,1,0:T(8,128)(2,1)S(1)} %copy-done.6, bf16[32,16,512]{2,1,0:T(8,128)(2,1)S(1)} %all-to-all-done.2.coarse_ref, f32[1,256]{1,0:T(1,128)S(1)} %get-tuple-element.46.gain_ref, bf16[512,256]{1,0:T(8,128)(2,1)S(1)} %copy.19.wqvt_ref, ...), custom_call_target="tpu_custom_call" | custom-call | flops 5000000000 | bytes 6293760 | tf_op jit(solution)/shard_map/third_layer/pallas_call | solution.py:273
  124.0 4.0 %all-to-all-start.3 = ((bf16[32,64,256]{2,1,0:T(8,128)(2,1)}), bf16[32,64,256]{2,1,0:T(8,128)(2,1)S(1)}, u32[]{:S(2)}, u32[]{:S(2)}) async-start(bf16[32,64,256]{2,1,0:T(8,128)(2,1)} %third_layer.1), calls=%async_computation.3 | async-start | bytes 2097152 | tf_op jit(solution)/shard_map/all_to_all | solution.py:290
  128.0 17.1 %all-to-all-done.3 = bf16[32,64,256]{2,1,0:T(8,128)(2,1)S(1)} async-done(((bf16[32,64,256]{2,1,0:T(8,128)(2,1)}), bf16[32,64,256]{2,1,0:T(8,128)(2,1)S(1)}, u32[]{:S(2)}, u32[]{:S(2)}) %all-to-all-start.3) | async-done | bytes 1048608 | tf_op jit(solution)/shard_map/all_to_all | solution.py:290
  145.1 1.6 %gather_fusion = bf16[32,64,256]{2,1,0:T(8,128)(2,1)} fusion(bf16[32,64,256]{2,1,0:T(8,128)(2,1)S(1)} %all-to-all-done.3, s32[1024]{0:T(1024)S(1)} %pad_clamp_fusion), kind=kCustom, calls=%fused_computation | custom fusion | bytes 2097280 | tf_op jit(solution)/shard_map/gather | solution.py:436
  (29 shorter events, 0.2 us)
Async XLA Ops:
  11.5 9.6 %copy-start.7 = (bf16[3,256,768]{2,1,0:T(8,128)(2,1)S(1)}, bf16[3,256,768]{2,1,0:T(8,128)(2,1)}, u32[]{:S(2)}) copy-start(bf16[3,256,768]{2,1,0:T(8,128)(2,1)} %wqkv_hbm.1) | copy-start | bytes 3538948
  11.5 26.6 %all-to-all-start = ((bf16[32,64,256]{2,1,0:T(8,128)(2,1)}), bf16[32,64,256]{2,1,0:T(8,128)(2,1)S(1)}, u32[]{:S(2)}, u32[]{:S(2)}) async-start(bf16[32,64,256]{2,1,0:T(8,128)(2,1)} %first_layer.1), calls=%async_computation | async-start | bytes 2097152 | tf_op jit(solution)/shard_map/all_to_all | solution.py:290
  21.1 0.7 copy-start.8
  21.1 1.0 copy-start.11
  21.1 1.8 %copy-start.9 = (f32[3,256]{1,0:T(4,128)S(1)}, f32[3,256]{1,0:T(4,128)}, u32[]{:S(2)}) copy-start(f32[3,256]{1,0:T(4,128)} %param.16) | copy-start | bytes 9220
  21.2 16.9 %copy-start.1 = (bf16[1024,512]{1,0:T(8,128)(2,1)S(1)}, bf16[1024,512]{1,0:T(8,128)(2,1)}, u32[]{:S(2)}) copy-start(bf16[1024,512]{1,0:T(8,128)(2,1)} %pool_ref.1) | copy-start | bytes 3145732
  38.1 15.5 %copy-start.10 = (s32[1,32]{1,0:T(1,128)S(1)}, s32[1,32]{1,0:T(1,128)}, u32[]{:S(2)}) copy-start(s32[1,32]{1,0:T(1,128)} %param.14) | copy-start | bytes 388
  48.6 1.0 copy-start.5
  49.5 28.5 %copy-start = (bf16[512,1536]{1,0:T(8,128)(2,1)S(1)}, bf16[512,1536]{1,0:T(8,128)(2,1)}, u32[]{:S(2)}) copy-start(bf16[512,1536]{1,0:T(8,128)(2,1)} %w_ref.5) | copy-start | bytes 4718596
  49.5 28.5 %copy-start.4 = (f32[512]{0:T(512)S(1)}, f32[512]{0:T(512)}, u32[]{:S(2)}) copy-start(f32[512]{0:T(512)} %param.20) | copy-start | bytes 6148
  49.5 15.6 %all-to-all-start.1 = ((bf16[32,16,512]{2,1,0:T(8,128)(2,1)}), bf16[32,16,512]{2,1,0:T(8,128)(2,1)S(1)}, u32[]{:S(2)}, u32[]{:S(2)}) async-start(bf16[32,16,512]{2,1,0:T(8,128)(2,1)} %get-tuple-element.25), calls=%async_computation.1 | async-start | bytes 1048576 | tf_op jit(solution)/shard_map/all_to_all | solution.py:290
  66.0 9.0 %collective-permute-start = (bf16[16,16,512]{2,1,0:T(8,128)(2,1)}, bf16[16,16,512]{2,1,0:T(8,128)(2,1)S(1)}, u32[]{:S(2)}, u32[]{:S(2)}) collective-permute-start(bf16[16,16,512]{2,1,0:T(8,128)(2,1)} %get-tuple-element.37), channel_id=1, source_target_pairs={{0,1},{1,2},{2,3},{3,0},{4,5},{5,6},{6,7},{7,4},{8,9},{9,10},{10,1... | collective-permute-start | bytes 786440 | tf_op jit(solution)/shard_map/ppermute | solution.py:386
  67.3 7.7 %collective-permute-start.3 = (bf16[16,16,512]{2,1,0:T(8,128)(2,1)}, bf16[16,16,512]{2,1,0:T(8,128)(2,1)S(1)}, u32[]{:S(2)}, u32[]{:S(2)}) collective-permute-start(bf16[16,16,512]{2,1,0:T(8,128)(2,1)} %get-tuple-element.36), channel_id=1, source_target_pairs={{0,3},{1,0},{2,1},{3,2},{4,7},{5,4},{6,5},{7,6},{8,11},{9,8},{10,9... | collective-permute-start | bytes 786440 | tf_op jit(solution)/shard_map/ppermute | solution.py:387
  68.8 11.9 %collective-permute-start.1 = (bf16[16,16,512]{2,1,0:T(8,128)(2,1)}, bf16[16,16,512]{2,1,0:T(8,128)(2,1)}, u32[]{:S(2)}, u32[]{:S(2)}) collective-permute-start(bf16[16,16,512]{2,1,0:T(8,128)(2,1)} %get-tuple-element.36), channel_id=1, source_target_pairs={{0,1},{1,2},{2,3},{3,0},{4,5},{5,6},{6,7},{7,4},{8,9},{9,10},{10,1... | collective-permute-start | bytes 786440 | tf_op jit(solution)/shard_map/ppermute | solution.py:388
  68.8 11.9 %collective-permute-start.2 = (bf16[16,16,512]{2,1,0:T(8,128)(2,1)}, bf16[16,16,512]{2,1,0:T(8,128)(2,1)}, u32[]{:S(2)}, u32[]{:S(2)}) collective-permute-start(bf16[16,16,512]{2,1,0:T(8,128)(2,1)} %get-tuple-element.37), channel_id=1, source_target_pairs={{0,3},{1,0},{2,1},{3,2},{4,7},{5,4},{6,5},{7,6},{8,11},{9,8},{10,9... | collective-permute-start | bytes 786440 | tf_op jit(solution)/shard_map/ppermute | solution.py:389
  75.0 11.2 %collective-permute-start.4 = (bf16[16,16,512]{2,1,0:T(8,128)(2,1)S(1)}, bf16[16,16,512]{2,1,0:T(8,128)(2,1)S(1)}, u32[]{:S(2)}, u32[]{:S(2)}) collective-permute-start(bf16[16,16,512]{2,1,0:T(8,128)(2,1)S(1)} %collective-permute-done.la_ref), channel_id=1, source_target_pairs={{0,1},{1,2},{2,3},{3,0},{4,5},{5,6},{6,7},{7,4},{8,9},{9,10},{10,1... | collective-permute-start | bytes 786440 | tf_op jit(solution)/shard_map/ppermute | solution.py:399
  75.0 11.2 %collective-permute-start.5 = (bf16[16,16,512]{2,1,0:T(8,128)(2,1)S(1)}, bf16[16,16,512]{2,1,0:T(8,128)(2,1)}, u32[]{:S(2)}, u32[]{:S(2)}) collective-permute-start(bf16[16,16,512]{2,1,0:T(8,128)(2,1)S(1)} %collective-permute-done.3.rb_ref), channel_id=1, source_target_pairs={{0,3},{1,0},{2,1},{3,2},{4,7},{5,4},{6,5},{7,6},{8,11},{9,8},{10,9... | collective-permute-start | bytes 786440 | tf_op jit(solution)/shard_map/ppermute | solution.py:400
  79.7 6.5 %copy-start.3 = (bf16[512,512]{1,0:T(8,128)(2,1)S(1)}, bf16[512,512]{1,0:T(8,128)(2,1)}, u32[]{:S(2)}) copy-start(bf16[512,512]{1,0:T(8,128)(2,1)} %wo_ref.1) | copy-start | bytes 1572868
  95.0 16.6 %copy-start.2 = (bf16[512,1024]{1,0:T(8,128)(2,1)S(1)}, bf16[512,1024]{1,0:T(8,128)(2,1)}, u32[]{:S(2)}) copy-start(bf16[512,1024]{1,0:T(8,128)(2,1)} %unpool_ref.1) | copy-start | bytes 3145732
  95.0 16.6 %all-to-all-start.2 = ((bf16[32,16,512]{2,1,0:T(8,128)(2,1)}), bf16[32,16,512]{2,1,0:T(8,128)(2,1)S(1)}, u32[]{:S(2)}, u32[]{:S(2)}) async-start(bf16[32,16,512]{2,1,0:T(8,128)(2,1)} %get-tuple-element.30), calls=%async_computation.2 | async-start | bytes 1048576 | tf_op jit(solution)/shard_map/all_to_all | solution.py:290
  111.6 1.2 copy-start.6
  124.0 21.1 %all-to-all-start.3 = ((bf16[32,64,256]{2,1,0:T(8,128)(2,1)}), bf16[32,64,256]{2,1,0:T(8,128)(2,1)S(1)}, u32[]{:S(2)}, u32[]{:S(2)}) async-start(bf16[32,64,256]{2,1,0:T(8,128)(2,1)} %third_layer.1), calls=%async_computation.3 | async-start | bytes 2097152 | tf_op jit(solution)/shard_map/all_to_all | solution.py:290

commit v2 on v1

--- a/solution.py
+++ b/solution.py
@@ -43,6 +43,7 @@
 SCALE = LOG2E / math.sqrt(32.0)
 BALLS = SUBS // 4
 VM = pltpu.VMEM
+HBM = pl.BlockSpec(memory_space=pltpu.HBM)
 
 
 def transposed(wqkv_ref, wqvt_ref):
@@ -50,7 +51,7 @@
     wqvt_ref[WIDTH:] = wqkv_ref[:, 2 * WIDTH :].T
 
 
-def fine_layer(load, reload, store, gain, wqvt_ref, wk_ref, wo_ref, scores, bufs, ready=None):
+def fine_layer(load, reload, store, send, gain, wqvt_ref, wk_ref, wo_ref, scores, bufs, ready=None):
     left, right = scores
     k_s, qt_s, vt_s, ot_s = bufs[0:2], bufs[2:4], bufs[4:6], bufs[6:8]
     masks = head_masks()
@@ -95,54 +96,92 @@
             soft(right, par, 1, i)
 
     def pair(t, carry):
+        if send is not None:
+
+            @pl.when(t >= 1)
+            def _():
+                send(2 * t - 2)
+
+            @pl.when(t >= 2)
+            def _():
+                send(2 * t - 3)
+
         step(2 * t, 0)
         step(2 * t + 1, 1)
         return carry
 
     lax.fori_loop(0, BALLS // 2, pair, 0)
+    if send is not None:
+        send(BALLS - 3)
+        send(BALLS - 2)
     finish(BALLS - 1, 1)
+    if send is not None:
+        send(BALLS - 1)
+
+
+def sent_to(staged, out, sem, at, to):
+    pltpu.make_async_copy(staged.at[at], out.at[to], sem).start()
+
+
+def all_sent(staged, out, sem):
+    pltpu.make_async_copy(staged, out, sem).wait()
 
 
 FINE_SCRATCH = [VM((4 * BALL, BALL), F32)] * 2 + [VM((BALL, WIDTH), BF16)] * 8
 
 
 def first_kernel(
-    rot, gain_ref, x_hbm, wqkv_hbm, wo_hbm, out_ref, wqvt_ref, x_ref, wqkv_ref, wo_ref, sems, *scratch
+    rot_hbm, gain_hbm, x_hbm, wqkv_hbm, wo_hbm, out_hbm,
+    rot, gain_ref, wqvt_ref, x_ref, wqkv_ref, wo_ref, staged, sems, *scratch
 ):
     groups = lax.axis_size("grp")
     device = lax.axis_index("pts") * groups + lax.axis_index("grp")
-    copies = [
-        pltpu.make_async_copy(wqkv_hbm.at[0], wqkv_ref, sems.at[0]),
-        pltpu.make_async_copy(x_hbm.at[pl.ds(0, 4)], x_ref.at[pl.ds(0, 4)], sems.at[1]),
-        pltpu.make_async_copy(wo_hbm.at[0], wo_ref, sems.at[2]),
+    weights = pltpu.make_async_copy(wqkv_hbm.at[0], wqkv_ref, sems.at[0])
+    early = pltpu.make_async_copy(x_hbm.at[pl.ds(0, 4)], x_ref.at[pl.ds(0, 4)], sems.at[1])
+    gains = pltpu.make_async_copy(gain_hbm, gain_ref, sems.at[2])
+    late = [
         pltpu.make_async_copy(x_hbm.at[pl.ds(4, SUBS - 4)], x_ref.at[pl.ds(4, SUBS - 4)], sems.at[3]),
+        pltpu.make_async_copy(wo_hbm.at[0], wo_ref, sems.at[4]),
+        pltpu.make_async_copy(rot_hbm, rot, sems.at[5]),
     ]
-    for copy in copies:
+    weights.start()
+    early.start()
+    gains.start()
+    weights.wait()
+    for copy in late:
         copy.start()
-    copies[0].wait()
     transposed(wqkv_ref, wqvt_ref)
-    copies[1].wait()
+    early.wait()
+    gains.wait()
 
     def ready():
-        copies[2].wait()
-        copies[3].wait()
+        for copy in late:
+            copy.wait()
 
     def load(b):
         return x_ref[pl.ds(4 * b, 4)].reshape(BALL, WIDTH).astype(F32)
 
     def store(b, y):
+        staged[pl.ds(4 * b, 4)] = y.reshape(4, SUB, WIDTH)
+
+    def send(b):
         for i in range(4):
-            out_ref[rot[device * SUBS + 4 * b + i] // (SUBS * groups)] = y[SUB * i : SUB * (i + 1)]
+            to = rot[device * SUBS + 4 * b + i] // (SUBS * groups)
+            sent_to(staged, out_hbm, sems.at[6], 4 * b + i, to)
 
     wk_ref = wqkv_ref.at[:, WIDTH : 2 * WIDTH]
     fine_layer(
-        load, load, store, gain_ref[...], wqvt_ref, wk_ref, wo_ref, scratch[:2], scratch[2:], ready
-    )
+        load, load, store, send, gain_ref[0:1], wqvt_ref, wk_ref, wo_ref, scratch[:2], scratch[2:], ready
+    )
+    all_sent(staged, out_hbm, sems.at[6])
 
 
 def second_kernel(
-    place, x_ref, gain_ref, wqvt_ref, wk_ref, wo_ref, pool_ref, out_ref, pooled_ref, wide_ref, *scratch
+    place, x_ref, gain_ref, wqkv_ref, wo_ref, pool_ref, out_ref, pooled_ref, wqvt_ref, wide_ref, *scratch
 ):
+    transposed(wqkv_ref, wqvt_ref)
+    wk_ref = wqkv_ref.at[:, WIDTH : 2 * WIDTH]
+
     def load(b):
         return jnp.concatenate([x_ref[place[4 * b + i]] for i in range(4)], axis=0).astype(F32)
 
@@ -159,13 +198,18 @@
         for i in range(4):
             pooled_ref[place[4 * b + i]] = pooled[POOL * i : POOL * (i + 1)]
 
-    fine_layer(load, load, store, gain_ref[...], wqvt_ref, wk_ref, wo_ref, scratch[:2], scratch[2:])
+    fine_layer(
+        load, load, store, None, gain_ref[1:2], wqvt_ref, wk_ref, wo_ref, scratch[:2], scratch[2:]
+    )
 
 
 def third_kernel(
-    place, x_ref, coarse_ref, gain_ref, wqvt_ref, wk_ref, wo_ref, unpool_ref, out_ref,
-    wide_ref, held_ref, *scratch
+    place, x_ref, coarse_ref, gain_ref, wqkv_ref, wo_ref, unpool_ref, out_ref,
+    wqvt_ref, wide_ref, held_ref, *scratch
 ):
+    transposed(wqkv_ref, wqvt_ref)
+    wk_ref = wqkv_ref.at[:, WIDTH : 2 * WIDTH]
+
     def load(b):
         coarse = jnp.concatenate([coarse_ref[place[4 * b + i]] for i in range(4)], axis=0)
         lifted = dot(coarse, unpool_ref[...])
@@ -184,7 +228,16 @@
         for i in range(4):
             out_ref[place[4 * b + i]] = y[SUB * i : SUB * (i + 1)]
 
-    fine_layer(load, reload, store, gain_ref[...], wqvt_ref, wk_ref, wo_ref, scratch[:2], scratch[2:])
+    fine_layer(
+        load, reload, store, None, gain_ref[2:3], wqvt_ref, wk_ref, wo_ref, scratch[:2], scratch[2:]
+    )
+
+
+def ordered_kernel(table, x_ref, out_hbm, sem):
+    me = lax.axis_index("grp")
+    for s in range(SUBS):
+        sent_to(x_ref, out_hbm, sem, table[me, s], s)
+    all_sent(x_ref, out_hbm, sem)
 
 
 def group_of(step):
@@ -212,7 +265,7 @@
 
 def coarse_kernel(
     table, blocks, counts, pooled_ref, own_ref, left_ref, right_ref, far_a_ref, far_b_ref,
-    gain_ref, w_ref, wo_ref, coarse_ref, sent_ref, kv_ref, all_ref, att_ref, a_ref, b_ref,
+    gain_ref, w_ref, wo_ref, coarse_hbm, sent_hbm, kv_ref, all_ref, att_ref, a_ref, b_ref, staged, sems,
 ):
     groups = lax.axis_size("grp")
     me = lax.axis_index("grp")
@@ -261,20 +314,27 @@
         soft(b_ref, b, 1)
         return carry
 
-    lax.fori_loop(0, count, block, 0)
-    result = (pooled_ref[...].astype(F32) + dot(att_ref[...], wo_ref[...])).astype(BF16)
-    coarse_ref[...] = result
-    for s in range(SUBS):
-        sent_ref[table[me, s]] = result[POOL * s : POOL * (s + 1)]
-
-
-def call(kernel, outs, scratch, args, tables=1, flops=0, exps=0, name=None, grant=16, specs=None):
+    lax.fori_loop(0, count, block, 0, unroll=2)
+    part = SUBS // 4
+    for c in range(4):
+        at = slice(part * POOL * c, part * POOL * (c + 1))
+        result = pooled_ref[at].astype(F32) + dot(att_ref[at], wo_ref[...])
+        staged[part * c : part * (c + 1)] = result.astype(BF16).reshape(part, POOL, CWIDTH)
+        near = pl.ds(part * c, part)
+        pltpu.make_async_copy(staged.at[near], coarse_hbm.at[near], sems.at[0]).start()
+        for s in range(part * c, part * (c + 1)):
+            sent_to(staged, sent_hbm, sems.at[1], s, table[me, s])
+    all_sent(staged, coarse_hbm, sems.at[0])
+    all_sent(staged, sent_hbm, sems.at[1])
+
+
+def call(kernel, outs, scratch, args, tables=1, flops=0, exps=0, name=None, grant=16, specs=None, out_specs=None):
     size = sum(a.size * a.dtype.itemsize for a in args)
     return pl.pallas_call(
         kernel,
         out_shape=outs,
         in_specs=specs or [SMEM] * tables + [VMEM] * (len(args) - tables),
-        out_specs=jax.tree.map(lambda _: VMEM, outs),
+        out_specs=jax.tree.map(lambda _: out_specs or VMEM, outs),
         scratch_shapes=scratch,
         name=name,
         compiler_params=pltpu.CompilerParams(vmem_limit_bytes=grant << 20),
@@ -346,17 +406,21 @@
         first_kernel,
         shaped(SUBS, SUB, width),
         [
+            pltpu.SMEM(rot_dest.shape, jnp.int32),
+            VM(fine_gain.shape, F32),
             VM((2 * width, width), BF16),
             VM((SUBS, SUB, width), BF16),
             VM((width, 3 * width), BF16),
             VM((width, width), BF16),
-            pltpu.SemaphoreType.DMA((4,)),
+            VM((SUBS, SUB, width), BF16),
+            pltpu.SemaphoreType.DMA((7,)),
         ]
         + FINE_SCRATCH,
-        (rot_dest, fine_gain[0:1], points.reshape(SUBS, SUB, width), fine_qkv, fine_out),
-        specs=[SMEM, VMEM] + [pl.BlockSpec(memory_space=pl.ANY)] * 3,
+        (rot_dest, fine_gain, points.reshape(SUBS, SUB, width), fine_qkv, fine_out),
+        specs=[HBM] * 5,
+        out_specs=HBM,
+        name="first_layer",
         grant=60,
-        name="first_layer",
         **cost,
     )
     sent, rot_dest, block_order, ball_sizes, fine_qkv, fine_out, fine_gain = lax.optimization_barrier(
@@ -364,18 +428,18 @@
     )
     targets, place = tables_of(rot_dest)
     members, lengths = ball_table(block_order[0], ball_sizes[0], crows // CBLK)
-    gains = [fine_gain[j : j + 1] for j in range(3)]
-    turned = [
-        jnp.concatenate([w[:, :width].T, w[:, 2 * width :].T], axis=0) for w in (fine_qkv[1], fine_qkv[2])
-    ]
-    keys = [w[:, width : 2 * width] for w in (fine_qkv[1], fine_qkv[2])]
+    packed = [fine_qkv[1], fine_qkv[2]]
+    outer = [fine_out[1], fine_out[2]]
 
     arrived = exchange(sent)
+    arrived, targets, place, members, lengths, packed, outer = lax.optimization_barrier(
+        (arrived, targets, place, members, lengths, packed, outer)
+    )
     second, pieces = call(
         second_kernel,
         (shaped(BALLS, BALL, width), shaped(SUBS, POOL, CWIDTH)),
-        [wide] + FINE_SCRATCH,
-        (place, arrived, gains[1], turned[0], keys[0], fine_out[1], pool_weight),
+        [VM((2 * width, width), BF16), wide] + FINE_SCRATCH,
+        (place, arrived, fine_gain, packed[0], outer[0], pool_weight),
         name="second_layer",
         **cost,
     )
@@ -408,33 +472,42 @@
     )
     coarse, pieces = call(
         coarse_kernel,
-        (shaped(crows, CWIDTH), shaped(SUBS, POOL, CWIDTH)),
+        (shaped(SUBS, POOL, CWIDTH), shaped(SUBS, POOL, CWIDTH)),
         [
             VM((groups * crows, 2 * CWIDTH), BF16),
             VM((SUBS, POOL, CWIDTH), BF16),
             VM((crows, CWIDTH), BF16),
             VM((4 * CBLK, MOST_BALL * CBLK), F32),
             VM((4 * CBLK, MOST_BALL * CBLK), F32),
+            VM((SUBS, POOL, CWIDTH), BF16),
+            pltpu.SemaphoreType.DMA((2,)),
         ],
         (targets, members, lengths, pooled, own, left, right, far_a, far_b, gain, coarse_qkv, coarse_out),
         tables=3,
         flops=4 * 10**9,
         exps=2 * 10**6,
         name="coarse_layer",
+        out_specs=HBM,
         grant=24,
     )
     pieces = exchange(pieces)
     sent = call(
         third_kernel,
         shaped(SUBS, SUB, width),
-        [wide, VM((BALLS, BALL, width), BF16)] + FINE_SCRATCH,
-        (place, second, pieces, gains[2], turned[1], keys[1], fine_out[2], unpool_weight),
+        [VM((2 * width, width), BF16), wide, VM((BALLS, BALL, width), BF16)] + FINE_SCRATCH,
+        (place, second, pieces, fine_gain, packed[1], outer[1], unpool_weight),
         name="third_layer",
         **cost,
     )
-    mine = lax.dynamic_index_in_dim(targets, lax.axis_index("grp"), 0, False)
-    refined = exchange(sent).at[mine].get(mode="promise_in_bounds", unique_indices=True)
-    return refined.reshape(rows, width), coarse
+    refined = call(
+        ordered_kernel,
+        shaped(SUBS, SUB, width),
+        [pltpu.SemaphoreType.DMA],
+        (targets, exchange(sent)),
+        out_specs=HBM,
+        name="ordered",
+    )
+    return refined.reshape(rows, width), coarse.reshape(crows, CWIDTH)
 
 
 def solution(mesh):

time: 147 us -> 141 us (0.959)
  blocking collectives: 0 us -> 52.3 us
  waiting for transfers between devices: 61.1 us -> 23.7 us
  starting transfers between devices: 30.8 us -> 18.5 us
  local copies, waits for them, and re-layouts: 8.08 us -> 1.54 us
  Pallas kernels: 44.1 us -> 41.8 us
    all_to_all x0 -> x3, blocking collectives: none -> 52.3 us  [exchange(): lax.all_to_all(pieces, 'pts', split_axis=0, concat_axis=0, tiled=True)]
    all_to_all x4 -> x1, waiting for transfers between devices: 53.7 us -> 13.9 us  [exchange(): lax.all_to_all(pieces, 'pts', split_axis=0, concat_axis=0, tiled=True)]
    all_to_all x4 -> x1, starting transfers between devices: 22.7 us -> 9.56 us  [exchange(): lax.all_to_all(pieces, 'pts', split_axis=0, concat_axis=0, tiled=True)]
    ppermute x1, waiting for transfers between devices: 3.34 us -> 0.01 us  [body(): left_a = lax.ppermute(pieces[:half], 'grp', up)]
    unnamed x24 -> x20, local copies, waits for them, and re-layouts: 2.82 us -> 0.06 us
    ppermute x1, waiting for transfers between devices: 1 us -> 3.65 us  [body(): left_b = lax.ppermute(pieces[half:], 'grp', up)]
    ppermute x1, waiting for transfers between devices: 0.01 us -> 2.57 us  [body(): right_b = lax.ppermute(pieces[half:], 'grp', down)]
    pallas_call x6 -> x7, Pallas kernels: 44.1 us -> 41.8 us  [call(): pl.pallas_call(kernel, out_shape=outs, in_specs=specs or [SMEM] * tables...]
  transfers between devices with their start and end apart: 10 -> 7, of which waited for: 7 -> 5; matrix products, arithmetic and copies ran while one was open for 2% -> 2% of each run, Pallas kernels for 3% -> 3%
where the time goes in v2:
time: 141 us; the launch traced here: 140 us
  blocking collectives  52.3 us (37%)
  Pallas kernels  41.8 us (30%)
  waiting for transfers between devices  23.7 us (17%)
  starting transfers between devices  18.5 us (13%)
  other arithmetic  1.64 us (1%)
  local copies, waits for them, and re-layouts  1.54 us (1%)
    all_to_all x3, blocking collectives, exchange(): lax.all_to_all(pieces, 'pts', split_axis=0, concat_axis=0, tiled=True)  52.3 us
    pallas_call x7, Pallas kernels, call(): pl.pallas_call(kernel, out_shape=outs, in_specs=specs or [SMEM] * tables...  41.8 us
    all_to_all x1, waiting for transfers between devices, exchange(): lax.all_to_all(pieces, 'pts', split_axis=0, concat_axis=0, tiled=True)  13.9 us
    all_to_all x1, starting transfers between devices, exchange(): lax.all_to_all(pieces, 'pts', split_axis=0, concat_axis=0, tiled=True)  9.56 us
    ppermute x1, waiting for transfers between devices, body(): left_b = lax.ppermute(pieces[half:], 'grp', up)  3.65 us
    ppermute x1, starting transfers between devices, body(): far_b = lax.ppermute(right_b, 'grp', down)  3.41 us
    ppermute x1, waiting for transfers between devices, body(): far_a = lax.ppermute(left_a, 'grp', up)  3.13 us
  transfers between devices with their start and end apart: 7, of which 5 were waited for; matrix products, arithmetic and copies ran while one was open for 2% of the time, Pallas kernels for 3%

profile of v2, /device:TPU:1, one launch (start us, length us, event | category | flops | bytes accessed | tf_op | source)
XLA Modules:
  0.0 140.5 jit_solution(14561029187015916844)
XLA Ops:
  0.6 8.7 %first_layer.1 = bf16[32,64,256]{2,1,0:T(8,128)(2,1)} custom-call(s32[4096]{0:T(1024)} %rot_hbm.1, f32[3,256]{1,0:T(4,128)} %gain_ref.1, bf16[32,64,256]{2,1,0:T(8,128)(2,1)} %bitcast.30, bf16[3,256,768]{2,1,0:T(8,128)(2,1)} %wqkv_hbm.1, bf16[3,256,256]{2,1,0:T(8,128)(2,1)} %wo_hbm.1), custom_call_target="tpu_custom_call" | custom-call | flops 5000000000 | bytes 5281792 | tf_op jit(solution)/shard_map/first_layer/pallas_call | solution.py:333
  9.3 0.0 copy-start.7
  9.3 0.0 copy-start.9
  9.3 0.0 copy-start.8
  9.3 0.0 copy-start.6
  9.4 9.6 %all-to-all-start = ((bf16[32,64,256]{2,1,0:T(8,128)(2,1)}), bf16[32,64,256]{2,1,0:T(8,128)(2,1)S(1)}, u32[]{:S(2)}, u32[]{:S(2)}) async-start(bf16[32,64,256]{2,1,0:T(8,128)(2,1)} %first_layer.1), calls=%async_computation | async-start | bytes 2097152 | tf_op jit(solution)/shard_map/all_to_all | solution.py:350
  18.9 0.0 copy-start.1
  18.9 0.0 copy-start.4
  19.0 0.0 copy-done.7
  19.0 0.1 reshape.61
  19.1 0.1 and_select_fusion
  19.2 0.0 copy-done.9
  19.2 0.1 select_reduce_fusion.5
  19.3 0.1 reshape.60.table
  19.4 0.0 copy-done.8
  19.4 0.2 select_reduce_fusion.4
  19.6 0.2 select_reduce_fusion.2
  19.8 0.1 add_minimum_fusion
  19.8 0.3 select_reduce_fusion.1
  20.1 0.1 reshape.62.blocks
  20.2 0.7 select_reduce_fusion.place
  20.9 1.2 slice_bitcast_fusion
  22.1 13.9 %all-to-all-done.x_ref = bf16[32,64,256]{2,1,0:T(8,128)(2,1)S(1)} async-done(((bf16[32,64,256]{2,1,0:T(8,128)(2,1)}), bf16[32,64,256]{2,1,0:T(8,128)(2,1)S(1)}, u32[]{:S(2)}, u32[]{:S(2)}) %all-to-all-start) | async-done | bytes 1048608 | tf_op jit(solution)/shard_map/all_to_all | solution.py:350
  36.0 0.0 copy-done.4
  36.0 9.8 %second_layer.1 = (bf16[8,256,256]{2,1,0:T(8,128)(2,1)S(1)}, bf16[32,16,512]{2,1,0:T(8,128)(2,1)S(1)}) custom-call(s32[32]{0:T(128)S(1)} %select_reduce_fusion.place, bf16[32,64,256]{2,1,0:T(8,128)(2,1)S(1)} %all-to-all-done.x_ref, f32[3,256]{1,0:T(4,128)S(1)} %copy-done.4, bf16[256,768]{1,0:T(8,128)(2,1)S(1)} %get-tuple-element.36.wqkv_ref, ...), custom_call_target="tpu_custom_call" | custom-call | flops 5000000000 | bytes 5249280 | tf_op jit(solution)/shard_map/second_layer/pallas_call | solution.py:333
  45.8 0.0 copy-start
  45.8 0.0 copy-start.5
  45.8 15.2 %all_to_all.20.pieces_ref = bf16[32,16,512]{2,1,0:T(8,128)(2,1)S(1)} all-to-all(bf16[32,16,512]{2,1,0:T(8,128)(2,1)S(1)} %get-tuple-element.41), channel_id=1, replica_groups=mesh['pts'=32,'grp'=4] {'pts'}, dimensions={0} | all-to-all | bytes 1048576 | tf_op jit(solution)/shard_map/all_to_all | solution.py:350
  61.0 2.8 %collective-permute-start.3 = (bf16[16,16,512]{2,1,0:T(8,128)(2,1)S(1)}, bf16[16,16,512]{2,1,0:T(8,128)(2,1)S(1)}, u32[]{:S(2)}, u32[]{:S(2)}) collective-permute-start(bf16[16,16,512]{2,1,0:T(8,128)(2,1)S(1)} %get-tuple-element.54), channel_id=1, source_target_pairs={{0,3},{1,0},{2,1},{3,2},{4,7},{5,4},{6,5},{7,6},{8,11},{9,8},{10,9... | collective-permute-start | bytes 786440 | tf_op jit(solution)/shard_map/ppermute | solution.py:451
  63.8 0.0 collective-permute-start
  63.8 0.0 collective-permute-start.1
  63.8 2.7 %collective-permute-start.2 = (bf16[16,16,512]{2,1,0:T(8,128)(2,1)S(1)}, bf16[16,16,512]{2,1,0:T(8,128)(2,1)S(1)}, u32[]{:S(2)}, u32[]{:S(2)}) collective-permute-start(bf16[16,16,512]{2,1,0:T(8,128)(2,1)S(1)} %get-tuple-element.55), channel_id=1, source_target_pairs={{0,3},{1,0},{2,1},{3,2},{4,7},{5,4},{6,5},{7,6},{8,11},{9,8},{10,9... | collective-permute-start | bytes 786440 | tf_op jit(solution)/shard_map/ppermute | solution.py:453
  66.5 2.6 %collective-permute-done.3.rb_ref = bf16[16,16,512]{2,1,0:T(8,128)(2,1)S(1)} collective-permute-done((bf16[16,16,512]{2,1,0:T(8,128)(2,1)S(1)}, bf16[16,16,512]{2,1,0:T(8,128)(2,1)S(1)}, u32[]{:S(2)}, u32[]{:S(2)}) %collective-permute-start.3) | collective-permute-done | bytes 262176 | tf_op jit(solution)/shard_map/ppermute | solution.py:451
  69.1 3.4 %collective-permute-start.5 = (bf16[16,16,512]{2,1,0:T(8,128)(2,1)S(1)}, bf16[16,16,512]{2,1,0:T(8,128)(2,1)S(1)}, u32[]{:S(2)}, u32[]{:S(2)}) collective-permute-start(bf16[16,16,512]{2,1,0:T(8,128)(2,1)S(1)} %collective-permute-done.3.rb_ref), channel_id=1, source_target_pairs={{0,3},{1,0},{2,1},{3,2},{4,7},{5,4},{6,5},{7,6},{8,11},{9,8},{10,9... | collective-permute-start | bytes 786440 | tf_op jit(solution)/shard_map/ppermute | solution.py:464
  72.5 0.0 collective-permute-done.la_ref
  72.5 0.0 collective-permute-start.4
  72.5 1.6 %own_projection.1 = (bf16[512,512]{1,0:T(8,128)(2,1)S(1)}, bf16[512,1536]{1,0:T(8,128)(2,1)S(1)}) custom-call(s32[4,32]{1,0:T(4,128)S(1)} %reshape.60.table, bf16[32,16,512]{2,1,0:T(8,128)(2,1)S(1)} %all_to_all.20.pieces_ref, f32[1,512]{1,0:T(1,128)S(1)} %bitcast.21, bf16[512,1536]{1,0:T(8,128)(2,1)S(1)} %copy-done), custom_call_target="tpu_custom_call" | custom-call | flops 805306368 | bytes 4199424 | tf_op jit(solution)/shard_map/own_projection/pallas_call | solution.py:333
  74.2 0.0 copy-start.3
  74.2 3.7 %collective-permute-done.1.lb_ref = bf16[16,16,512]{2,1,0:T(8,128)(2,1)S(1)} collective-permute-done((bf16[16,16,512]{2,1,0:T(8,128)(2,1)S(1)}, bf16[16,16,512]{2,1,0:T(8,128)(2,1)S(1)}, u32[]{:S(2)}, u32[]{:S(2)}) %collective-permute-start.1) | collective-permute-done | bytes 262176 | tf_op jit(solution)/shard_map/ppermute | solution.py:452
  77.8 0.0 collective-permute-done.2.ra_ref
  77.8 2.0 %near_projection.1 = (bf16[512,1024]{1,0:T(8,128)(2,1)S(1)}, bf16[512,1024]{1,0:T(8,128)(2,1)S(1)}) custom-call(s32[4,32]{1,0:T(4,128)S(1)} %reshape.60.table, bf16[16,16,512]{2,1,0:T(8,128)(2,1)S(1)} %collective-permute-done.la_ref, bf16[16,16,512]{2,1,0:T(8,128)(2,1)S(1)} %collective-permute-done.1.lb_ref, ...), custom_call_target="tpu_custom_call" | custom-call | flops 1073741824 | bytes 5248000 | tf_op jit(solution)/shard_map/near_projection/pallas_call | solution.py:333
  79.8 0.5 collective-permute-done.5.far_b_ref
  80.3 3.1 %collective-permute-done.4.far_a_ref = bf16[16,16,512]{2,1,0:T(8,128)(2,1)S(1)} collective-permute-done((bf16[16,16,512]{2,1,0:T(8,128)(2,1)S(1)}, bf16[16,16,512]{2,1,0:T(8,128)(2,1)S(1)}, u32[]{:S(2)}, u32[]{:S(2)}) %collective-permute-start.4) | collective-permute-done | bytes 262176 | tf_op jit(solution)/shard_map/ppermute | solution.py:463
  83.4 8.0 %coarse_layer.1 = (bf16[32,16,512]{2,1,0:T(8,128)(2,1)}, bf16[32,16,512]{2,1,0:T(8,128)(2,1)S(1)}) custom-call(s32[4,32]{1,0:T(4,128)S(1)} %reshape.60.table, s32[64]{0:T(128)S(1)} %reshape.62.blocks, s32[8]{0:T(128)S(1)} %get-tuple-element.40.counts, bf16[512,512]{1,0:T(8,128)(2,1)S(1)} %get-tuple-element.42.pooled_ref, ...), custom_call_target="tpu_custom_call" | custom-call | flops 4000000000 | bytes 13637184 | tf_op jit(solution)/shard_map/coarse_layer/pallas_call | solution.py:333
  91.4 16.5 %all_to_all.21.coarse_ref = bf16[32,16,512]{2,1,0:T(8,128)(2,1)S(1)} all-to-all(bf16[32,16,512]{2,1,0:T(8,128)(2,1)S(1)} %get-tuple-element.46), channel_id=1, replica_groups=mesh['pts'=32,'grp'=4] {'pts'}, dimensions={0} | all-to-all | bytes 1048576 | tf_op jit(solution)/shard_map/all_to_all | solution.py:350
  107.9 10.2 %third_layer.1 = bf16[32,64,256]{2,1,0:T(8,128)(2,1)S(1)} custom-call(s32[32]{0:T(128)S(1)} %select_reduce_fusion.place, bf16[8,256,256]{2,1,0:T(8,128)(2,1)S(1)} %get-tuple-element.38.x_ref, bf16[32,16,512]{2,1,0:T(8,128)(2,1)S(1)} %all_to_all.21.coarse_ref, f32[3,256]{1,0:T(4,128)S(1)} %copy-done.4, bf16[256,768]{1,0:T(8,128)(2,1)S(1)} %get-tuple-element.47.wqkv_ref, ...), custom_call_target="tpu_custom_call" | custom-call | flops 5000000000 | bytes 6297856 | tf_op jit(solution)/shard_map/third_layer/pallas_call | solution.py:333
  118.1 20.7 %all_to_all.22.x_ref = bf16[32,64,256]{2,1,0:T(8,128)(2,1)S(1)} all-to-all(bf16[32,64,256]{2,1,0:T(8,128)(2,1)S(1)} %third_layer.1), channel_id=1, replica_groups=mesh['pts'=32,'grp'=4] {'pts'}, dimensions={0} | all-to-all | bytes 2097152 | tf_op jit(solution)/shard_map/all_to_all | solution.py:350
  138.8 1.5 %ordered.1 = bf16[32,64,256]{2,1,0:T(8,128)(2,1)} custom-call(s32[4,32]{1,0:T(4,128)S(1)} %reshape.60.table, bf16[32,64,256]{2,1,0:T(8,128)(2,1)S(1)} %all_to_all.22.x_ref), custom_call_target="tpu_custom_call" | custom-call | bytes 2098176 | tf_op jit(solution)/shard_map/ordered/pallas_call | solution.py:333
  (12 shorter events, 0.1 us)
Async XLA Ops:
  9.3 9.7 %copy-start.7 = (s32[4096]{0:T(1024)S(1)}, s32[4096]{0:T(1024)}, u32[]{:S(2)}) copy-start(s32[4096]{0:T(1024)} %rot_hbm.1) | copy-start | bytes 49156
  9.3 9.9 %copy-start.9 = (s32[1,8]{1,0:T(1,128)S(1)}, s32[1,8]{1,0:T(1,128)}, u32[]{:S(2)}) copy-start(s32[1,8]{1,0:T(1,128)} %param.15) | copy-start | bytes 100
  9.3 10.1 %copy-start.8 = (s32[1,32]{1,0:T(1,128)S(1)}, s32[1,32]{1,0:T(1,128)}, u32[]{:S(2)}) copy-start(s32[1,32]{1,0:T(1,128)} %param.14) | copy-start | bytes 388
  9.3 11.6 %copy-start.6 = (bf16[3,256,256]{2,1,0:T(8,128)(2,1)S(1)}, bf16[3,256,256]{2,1,0:T(8,128)(2,1)}, u32[]{:S(2)}) copy-start(bf16[3,256,256]{2,1,0:T(8,128)(2,1)} %wo_hbm.1) | copy-start | bytes 1179652
  9.4 26.6 %all-to-all-start = ((bf16[32,64,256]{2,1,0:T(8,128)(2,1)}), bf16[32,64,256]{2,1,0:T(8,128)(2,1)S(1)}, u32[]{:S(2)}, u32[]{:S(2)}) async-start(bf16[32,64,256]{2,1,0:T(8,128)(2,1)} %first_layer.1), calls=%async_computation | async-start | bytes 2097152 | tf_op jit(solution)/shard_map/all_to_all | solution.py:350
  18.9 17.1 %copy-start.1 = (bf16[1024,512]{1,0:T(8,128)(2,1)S(1)}, bf16[1024,512]{1,0:T(8,128)(2,1)}, u32[]{:S(2)}) copy-start(bf16[1024,512]{1,0:T(8,128)(2,1)} %pool_ref.1) | copy-start | bytes 3145732
  18.9 17.0 %copy-start.4 = (f32[3,256]{1,0:T(4,128)S(1)}, f32[3,256]{1,0:T(4,128)}, u32[]{:S(2)}) copy-start(f32[3,256]{1,0:T(4,128)} %gain_ref.1) | copy-start | bytes 9220
  45.8 26.7 %copy-start = (bf16[512,1536]{1,0:T(8,128)(2,1)S(1)}, bf16[512,1536]{1,0:T(8,128)(2,1)}, u32[]{:S(2)}) copy-start(bf16[512,1536]{1,0:T(8,128)(2,1)} %w_ref.5) | copy-start | bytes 4718596
  45.8 26.7 %copy-start.5 = (f32[512]{0:T(512)S(1)}, f32[512]{0:T(512)}, u32[]{:S(2)}) copy-start(f32[512]{0:T(512)} %param.20) | copy-start | bytes 6148
  61.0 8.1 %collective-permute-start.3 = (bf16[16,16,512]{2,1,0:T(8,128)(2,1)S(1)}, bf16[16,16,512]{2,1,0:T(8,128)(2,1)S(1)}, u32[]{:S(2)}, u32[]{:S(2)}) collective-permute-start(bf16[16,16,512]{2,1,0:T(8,128)(2,1)S(1)} %get-tuple-element.54), channel_id=1, source_target_pairs={{0,3},{1,0},{2,1},{3,2},{4,7},{5,4},{6,5},{7,6},{8,11},{9,8},{10,9... | collective-permute-start | bytes 786440 | tf_op jit(solution)/shard_map/ppermute | solution.py:451
  63.8 8.7 %collective-permute-start = (bf16[16,16,512]{2,1,0:T(8,128)(2,1)S(1)}, bf16[16,16,512]{2,1,0:T(8,128)(2,1)S(1)}, u32[]{:S(2)}, u32[]{:S(2)}) collective-permute-start(bf16[16,16,512]{2,1,0:T(8,128)(2,1)S(1)} %get-tuple-element.55), channel_id=1, source_target_pairs={{0,1},{1,2},{2,3},{3,0},{4,5},{5,6},{6,7},{7,4},{8,9},{9,10},{10,1... | collective-permute-start | bytes 786440 | tf_op jit(solution)/shard_map/ppermute | solution.py:450
  63.8 14.0 %collective-permute-start.1 = (bf16[16,16,512]{2,1,0:T(8,128)(2,1)S(1)}, bf16[16,16,512]{2,1,0:T(8,128)(2,1)S(1)}, u32[]{:S(2)}, u32[]{:S(2)}) collective-permute-start(bf16[16,16,512]{2,1,0:T(8,128)(2,1)S(1)} %get-tuple-element.54), channel_id=1, source_target_pairs={{0,1},{1,2},{2,3},{3,0},{4,5},{5,6},{6,7},{7,4},{8,9},{9,10},{10,1... | collective-permute-start | bytes 786440 | tf_op jit(solution)/shard_map/ppermute | solution.py:452
  63.8 14.0 %collective-permute-start.2 = (bf16[16,16,512]{2,1,0:T(8,128)(2,1)S(1)}, bf16[16,16,512]{2,1,0:T(8,128)(2,1)S(1)}, u32[]{:S(2)}, u32[]{:S(2)}) collective-permute-start(bf16[16,16,512]{2,1,0:T(8,128)(2,1)S(1)} %get-tuple-element.55), channel_id=1, source_target_pairs={{0,3},{1,0},{2,1},{3,2},{4,7},{5,4},{6,5},{7,6},{8,11},{9,8},{10,9... | collective-permute-start | bytes 786440 | tf_op jit(solution)/shard_map/ppermute | solution.py:453
  69.1 11.2 %collective-permute-start.5 = (bf16[16,16,512]{2,1,0:T(8,128)(2,1)S(1)}, bf16[16,16,512]{2,1,0:T(8,128)(2,1)S(1)}, u32[]{:S(2)}, u32[]{:S(2)}) collective-permute-start(bf16[16,16,512]{2,1,0:T(8,128)(2,1)S(1)} %collective-permute-done.3.rb_ref), channel_id=1, source_target_pairs={{0,3},{1,0},{2,1},{3,2},{4,7},{5,4},{6,5},{7,6},{8,11},{9,8},{10,9... | collective-permute-start | bytes 786440 | tf_op jit(solution)/shard_map/ppermute | solution.py:464
  72.5 11.0 %collective-permute-start.4 = (bf16[16,16,512]{2,1,0:T(8,128)(2,1)S(1)}, bf16[16,16,512]{2,1,0:T(8,128)(2,1)S(1)}, u32[]{:S(2)}, u32[]{:S(2)}) collective-permute-start(bf16[16,16,512]{2,1,0:T(8,128)(2,1)S(1)} %collective-permute-done.la_ref), channel_id=1, source_target_pairs={{0,1},{1,2},{2,3},{3,0},{4,5},{5,6},{6,7},{7,4},{8,9},{9,10},{10,1... | collective-permute-start | bytes 786440 | tf_op jit(solution)/shard_map/ppermute | solution.py:463
  74.2 9.3 %copy-start.3 = (bf16[512,512]{1,0:T(8,128)(2,1)S(1)}, bf16[512,512]{1,0:T(8,128)(2,1)}, u32[]{:S(2)}) copy-start(bf16[512,512]{1,0:T(8,128)(2,1)} %wo_ref.1) | copy-start | bytes 1572868
  83.4 24.5 %copy-start.2 = (bf16[512,1024]{1,0:T(8,128)(2,1)S(1)}, bf16[512,1024]{1,0:T(8,128)(2,1)}, u32[]{:S(2)}) copy-start(bf16[512,1024]{1,0:T(8,128)(2,1)} %unpool_ref.1) | copy-start | bytes 3145732

commit v3 on v2

--- a/solution.py
+++ b/solution.py
@@ -177,7 +177,7 @@
 
 
 def second_kernel(
-    place, x_ref, gain_ref, wqkv_ref, wo_ref, pool_ref, out_ref, pooled_ref, wqvt_ref, wide_ref, *scratch
+    place, x_ref, gain_ref, wqkv_ref, wo_ref, pool_ref, out_ref, pooled_ref, wqvt_ref, wide_ref, rows_ref, *scratch
 ):
     transposed(wqkv_ref, wqvt_ref)
     wk_ref = wqkv_ref.at[:, WIDTH : 2 * WIDTH]
@@ -190,33 +190,39 @@
         wide = y.astype(F32)
         for c in range(2):
             wide_ref[c] = wide[:, 128 * c : 128 * c + 128]
-        rows = jnp.concatenate(
+        rows_ref[b] = jnp.concatenate(
             [wide_ref[c, pl.ds(j, BALL // 4, stride=4)] for j in range(4) for c in range(2)],
             axis=1,
         ).astype(BF16)
-        pooled = dot(rows, pool_ref[...]).astype(BF16)
-        for i in range(4):
-            pooled_ref[place[4 * b + i]] = pooled[POOL * i : POOL * (i + 1)]
 
     fine_layer(
         load, load, store, None, gain_ref[1:2], wqvt_ref, wk_ref, wo_ref, scratch[:2], scratch[2:]
     )
+    part = BALLS // 2
+    for b in range(0, BALLS, part):
+        rows = rows_ref[b : b + part].reshape(part * BALL // 4, 4 * WIDTH)
+        pooled = dot(rows, pool_ref[...]).astype(BF16)
+        for i in range(4 * part):
+            pooled_ref[place[4 * b + i]] = pooled[POOL * i : POOL * (i + 1)]
 
 
 def third_kernel(
     place, x_ref, coarse_ref, gain_ref, wqkv_ref, wo_ref, unpool_ref, out_ref,
-    wqvt_ref, wide_ref, held_ref, *scratch
+    wqvt_ref, wide_ref, lifted_ref, held_ref, *scratch
 ):
     transposed(wqkv_ref, wqvt_ref)
     wk_ref = wqkv_ref.at[:, WIDTH : 2 * WIDTH]
 
+    part = BALLS // 2
+    for b in range(0, BALLS, part):
+        coarse = jnp.concatenate([coarse_ref[place[4 * b + i]] for i in range(4 * part)], axis=0)
+        lifted_ref[b : b + part] = dot(coarse, unpool_ref[...]).reshape(part, BALL // 4, 4 * WIDTH)
+
     def load(b):
-        coarse = jnp.concatenate([coarse_ref[place[4 * b + i]] for i in range(4)], axis=0)
-        lifted = dot(coarse, unpool_ref[...])
         for j in range(4):
             for c in range(2):
                 at = WIDTH * j + 128 * c
-                wide_ref[c, pl.ds(j, BALL // 4, stride=4)] = lifted[:, at : at + 128]
+                wide_ref[c, pl.ds(j, BALL // 4, stride=4)] = lifted_ref[b, :, at : at + 128]
         x = x_ref[b].astype(F32) + jnp.concatenate([wide_ref[0], wide_ref[1]], axis=1)
         held_ref[b] = x.astype(BF16)
         return x.astype(BF16).astype(F32)
@@ -265,7 +271,7 @@
 
 def coarse_kernel(
     table, blocks, counts, pooled_ref, own_ref, left_ref, right_ref, far_a_ref, far_b_ref,
-    gain_ref, w_ref, wo_ref, coarse_hbm, sent_hbm, kv_ref, all_ref, att_ref, a_ref, b_ref, staged, sems,
+    gain_ref, w_ref, wo_ref, coarse_hbm, sent_ref, kv_ref, all_ref, att_ref, a_ref, b_ref, staged, sem,
 ):
     groups = lax.axis_size("grp")
     me = lax.axis_index("grp")
@@ -319,13 +325,13 @@
     for c in range(4):
         at = slice(part * POOL * c, part * POOL * (c + 1))
         result = pooled_ref[at].astype(F32) + dot(att_ref[at], wo_ref[...])
-        staged[part * c : part * (c + 1)] = result.astype(BF16).reshape(part, POOL, CWIDTH)
+        result = result.astype(BF16).reshape(part, POOL, CWIDTH)
+        staged[part * c : part * (c + 1)] = result
         near = pl.ds(part * c, part)
-        pltpu.make_async_copy(staged.at[near], coarse_hbm.at[near], sems.at[0]).start()
-        for s in range(part * c, part * (c + 1)):
-            sent_to(staged, sent_hbm, sems.at[1], s, table[me, s])
-    all_sent(staged, coarse_hbm, sems.at[0])
-    all_sent(staged, sent_hbm, sems.at[1])
+        pltpu.make_async_copy(staged.at[near], coarse_hbm.at[near], sem).start()
+        for s in range(part):
+            sent_ref[table[me, part * c + s]] = result[s]
+    all_sent(staged, coarse_hbm, sem)
 
 
 def call(kernel, outs, scratch, args, tables=1, flops=0, exps=0, name=None, grant=16, specs=None, out_specs=None):
@@ -334,7 +340,7 @@
         kernel,
         out_shape=outs,
         in_specs=specs or [SMEM] * tables + [VMEM] * (len(args) - tables),
-        out_specs=jax.tree.map(lambda _: out_specs or VMEM, outs),
+        out_specs=out_specs if isinstance(out_specs, tuple) else jax.tree.map(lambda _: out_specs or VMEM, outs),
         scratch_shapes=scratch,
         name=name,
         compiler_params=pltpu.CompilerParams(vmem_limit_bytes=grant << 20),
@@ -438,7 +444,7 @@
     second, pieces = call(
         second_kernel,
         (shaped(BALLS, BALL, width), shaped(SUBS, POOL, CWIDTH)),
-        [VM((2 * width, width), BF16), wide] + FINE_SCRATCH,
+        [VM((2 * width, width), BF16), wide, VM((BALLS, BALL // 4, 4 * width), BF16)] + FINE_SCRATCH,
         (place, arrived, fine_gain, packed[0], outer[0], pool_weight),
         name="second_layer",
         **cost,
@@ -480,21 +486,27 @@
             VM((4 * CBLK, MOST_BALL * CBLK), F32),
             VM((4 * CBLK, MOST_BALL * CBLK), F32),
             VM((SUBS, POOL, CWIDTH), BF16),
-            pltpu.SemaphoreType.DMA((2,)),
+            pltpu.SemaphoreType.DMA,
         ],
         (targets, members, lengths, pooled, own, left, right, far_a, far_b, gain, coarse_qkv, coarse_out),
         tables=3,
         flops=4 * 10**9,
         exps=2 * 10**6,
         name="coarse_layer",
-        out_specs=HBM,
+        out_specs=(HBM, VMEM),
         grant=24,
     )
     pieces = exchange(pieces)
     sent = call(
         third_kernel,
         shaped(SUBS, SUB, width),
-        [VM((2 * width, width), BF16), wide, VM((BALLS, BALL, width), BF16)] + FINE_SCRATCH,
+        [
+            VM((2 * width, width), BF16),
+            wide,
+            VM((BALLS, BALL // 4, 4 * width), F32),
+            VM((BALLS, BALL, width), BF16),
+        ]
+        + FINE_SCRATCH,
         (place, second, pieces, fine_gain, packed[1], outer[1], unpool_weight),
         name="third_layer",
         **cost,

time: 141 us -> 135 us (0.957)
  Pallas kernels: 41.8 us -> 36.4 us
    pallas_call x7, Pallas kernels: 41.8 us -> 36.4 us  [call(): pl.pallas_call(kernel, out_shape=outs, in_specs=specs or [SMEM] * tables...]
where the time goes in v3:
time: 135 us
  blocking collectives  52.3 us (39%)
  Pallas kernels  36.4 us (27%)
  waiting for transfers between devices  23.7 us (18%)
  starting transfers between devices  18.5 us (14%)
  other arithmetic  1.64 us (1%)
  local copies, waits for them, and re-layouts  1.54 us (1%)
    all_to_all x3, blocking collectives, exchange(): lax.all_to_all(pieces, 'pts', split_axis=0, concat_axis=0, tiled=True)  52.3 us
    pallas_call x7, Pallas kernels, call(): pl.pallas_call(kernel, out_shape=outs, in_specs=specs or [SMEM] * tables...  36.4 us
    all_to_all x1, waiting for transfers between devices, exchange(): lax.all_to_all(pieces, 'pts', split_axis=0, concat_axis=0, tiled=True)  13.9 us
    all_to_all x1, starting transfers between devices, exchange(): lax.all_to_all(pieces, 'pts', split_axis=0, concat_axis=0, tiled=True)  9.56 us
    ppermute x1, waiting for transfers between devices, body(): left_b = lax.ppermute(pieces[half:], 'grp', up)  3.65 us
    ppermute x1, starting transfers between devices, body(): far_b = lax.ppermute(right_b, 'grp', down)  3.41 us
    ppermute x1, waiting for transfers between devices, body(): far_a = lax.ppermute(left_a, 'grp', up)  3.13 us
    ppermute x1, starting transfers between devices, body(): right_b = lax.ppermute(pieces[half:], 'grp', down)  2.81 us
  transfers between devices with their start and end apart: 7, of which 5 were waited for; matrix products, arithmetic and copies ran while one was open for 2% of the time, Pallas kernels for 3%

profile of v3, /device:TPU:1, one launch (start us, length us, event | category | flops | bytes accessed | tf_op | source)
XLA Modules:
  0.0 135.0 jit_solution(13458730706354378049)
XLA Ops:
  0.6 8.7 %first_layer.1 = bf16[32,64,256]{2,1,0:T(8,128)(2,1)} custom-call(s32[4096]{0:T(1024)} %rot_hbm.1, f32[3,256]{1,0:T(4,128)} %gain_ref.1, bf16[32,64,256]{2,1,0:T(8,128)(2,1)} %bitcast.30, bf16[3,256,768]{2,1,0:T(8,128)(2,1)} %wqkv_hbm.1, bf16[3,256,256]{2,1,0:T(8,128)(2,1)} %wo_hbm.1), custom_call_target="tpu_custom_call" | custom-call | flops 5000000000 | bytes 5281792 | tf_op jit(solution)/shard_map/first_layer/pallas_call | solution.py:339
  9.3 0.0 copy-start.7
  9.3 0.0 copy-start.9
  9.3 0.0 copy-start.8
  9.3 0.0 copy-start.6
  9.4 9.6 %all-to-all-start = ((bf16[32,64,256]{2,1,0:T(8,128)(2,1)}), bf16[32,64,256]{2,1,0:T(8,128)(2,1)S(1)}, u32[]{:S(2)}, u32[]{:S(2)}) async-start(bf16[32,64,256]{2,1,0:T(8,128)(2,1)} %first_layer.1), calls=%async_computation | async-start | bytes 2097152 | tf_op jit(solution)/shard_map/all_to_all | solution.py:356
  18.9 0.0 copy-start.1
  18.9 0.0 copy-start.4
  19.0 0.0 copy-done.7
  19.0 0.1 reshape.61
  19.1 0.1 and_select_fusion
  19.2 0.0 copy-done.9
  19.2 0.1 select_reduce_fusion.5
  19.3 0.1 reshape.60.table
  19.4 0.0 copy-done.8
  19.4 0.2 select_reduce_fusion.4
  19.6 0.2 select_reduce_fusion.2
  19.8 0.1 add_minimum_fusion
  19.8 0.3 select_reduce_fusion.1
  20.1 0.1 reshape.62.blocks
  20.2 0.7 select_reduce_fusion.place
  20.9 1.2 slice_bitcast_fusion
  22.1 13.9 %all-to-all-done.x_ref = bf16[32,64,256]{2,1,0:T(8,128)(2,1)S(1)} async-done(((bf16[32,64,256]{2,1,0:T(8,128)(2,1)}), bf16[32,64,256]{2,1,0:T(8,128)(2,1)S(1)}, u32[]{:S(2)}, u32[]{:S(2)}) %all-to-all-start) | async-done | bytes 1048608 | tf_op jit(solution)/shard_map/all_to_all | solution.py:356
  36.0 0.0 copy-done.4
  36.0 8.0 %second_layer.1 = (bf16[8,256,256]{2,1,0:T(8,128)(2,1)S(1)}, bf16[32,16,512]{2,1,0:T(8,128)(2,1)S(1)}) custom-call(s32[32]{0:T(128)S(1)} %select_reduce_fusion.place, bf16[32,64,256]{2,1,0:T(8,128)(2,1)S(1)} %all-to-all-done.x_ref, f32[3,256]{1,0:T(4,128)S(1)} %copy-done.4, bf16[256,768]{1,0:T(8,128)(2,1)S(1)} %get-tuple-element.36.wqkv_ref, ...), custom_call_target="tpu_custom_call" | custom-call | flops 5000000000 | bytes 5249280 | tf_op jit(solution)/shard_map/second_layer/pallas_call | solution.py:339
  44.0 0.0 copy-start
  44.0 0.0 copy-start.5
  44.0 15.2 %all_to_all.20.pieces_ref = bf16[32,16,512]{2,1,0:T(8,128)(2,1)S(1)} all-to-all(bf16[32,16,512]{2,1,0:T(8,128)(2,1)S(1)} %get-tuple-element.41), channel_id=1, replica_groups=mesh['pts'=32,'grp'=4] {'pts'}, dimensions={0} | all-to-all | bytes 1048576 | tf_op jit(solution)/shard_map/all_to_all | solution.py:356
  59.2 2.8 %collective-permute-start.3 = (bf16[16,16,512]{2,1,0:T(8,128)(2,1)S(1)}, bf16[16,16,512]{2,1,0:T(8,128)(2,1)S(1)}, u32[]{:S(2)}, u32[]{:S(2)}) collective-permute-start(bf16[16,16,512]{2,1,0:T(8,128)(2,1)S(1)} %get-tuple-element.54), channel_id=1, source_target_pairs={{0,3},{1,0},{2,1},{3,2},{4,7},{5,4},{6,5},{7,6},{8,11},{9,8},{10,9... | collective-permute-start | bytes 786440 | tf_op jit(solution)/shard_map/ppermute | solution.py:457
  62.0 0.0 collective-permute-start
  62.0 0.0 collective-permute-start.1
  62.0 2.7 %collective-permute-start.2 = (bf16[16,16,512]{2,1,0:T(8,128)(2,1)S(1)}, bf16[16,16,512]{2,1,0:T(8,128)(2,1)S(1)}, u32[]{:S(2)}, u32[]{:S(2)}) collective-permute-start(bf16[16,16,512]{2,1,0:T(8,128)(2,1)S(1)} %get-tuple-element.55), channel_id=1, source_target_pairs={{0,3},{1,0},{2,1},{3,2},{4,7},{5,4},{6,5},{7,6},{8,11},{9,8},{10,9... | collective-permute-start | bytes 786440 | tf_op jit(solution)/shard_map/ppermute | solution.py:459
  64.7 2.6 %collective-permute-done.3.rb_ref = bf16[16,16,512]{2,1,0:T(8,128)(2,1)S(1)} collective-permute-done((bf16[16,16,512]{2,1,0:T(8,128)(2,1)S(1)}, bf16[16,16,512]{2,1,0:T(8,128)(2,1)S(1)}, u32[]{:S(2)}, u32[]{:S(2)}) %collective-permute-start.3) | collective-permute-done | bytes 262176 | tf_op jit(solution)/shard_map/ppermute | solution.py:457
  67.3 3.4 %collective-permute-start.5 = (bf16[16,16,512]{2,1,0:T(8,128)(2,1)S(1)}, bf16[16,16,512]{2,1,0:T(8,128)(2,1)S(1)}, u32[]{:S(2)}, u32[]{:S(2)}) collective-permute-start(bf16[16,16,512]{2,1,0:T(8,128)(2,1)S(1)} %collective-permute-done.3.rb_ref), channel_id=1, source_target_pairs={{0,3},{1,0},{2,1},{3,2},{4,7},{5,4},{6,5},{7,6},{8,11},{9,8},{10,9... | collective-permute-start | bytes 786440 | tf_op jit(solution)/shard_map/ppermute | solution.py:470
  70.7 0.0 collective-permute-done.la_ref
  70.7 0.0 collective-permute-start.4
  70.7 1.7 %own_projection.1 = (bf16[512,512]{1,0:T(8,128)(2,1)S(1)}, bf16[512,1536]{1,0:T(8,128)(2,1)S(1)}) custom-call(s32[4,32]{1,0:T(4,128)S(1)} %reshape.60.table, bf16[32,16,512]{2,1,0:T(8,128)(2,1)S(1)} %all_to_all.20.pieces_ref, f32[1,512]{1,0:T(1,128)S(1)} %bitcast.21, bf16[512,1536]{1,0:T(8,128)(2,1)S(1)} %copy-done), custom_call_target="tpu_custom_call" | custom-call | flops 805306368 | bytes 4199424 | tf_op jit(solution)/shard_map/own_projection/pallas_call | solution.py:339
  72.4 0.0 copy-start.3
  72.4 3.6 %collective-permute-done.1.lb_ref = bf16[16,16,512]{2,1,0:T(8,128)(2,1)S(1)} collective-permute-done((bf16[16,16,512]{2,1,0:T(8,128)(2,1)S(1)}, bf16[16,16,512]{2,1,0:T(8,128)(2,1)S(1)}, u32[]{:S(2)}, u32[]{:S(2)}) %collective-permute-start.1) | collective-permute-done | bytes 262176 | tf_op jit(solution)/shard_map/ppermute | solution.py:458
  76.0 0.0 collective-permute-done.2.ra_ref
  76.0 2.0 %near_projection.1 = (bf16[512,1024]{1,0:T(8,128)(2,1)S(1)}, bf16[512,1024]{1,0:T(8,128)(2,1)S(1)}) custom-call(s32[4,32]{1,0:T(4,128)S(1)} %reshape.60.table, bf16[16,16,512]{2,1,0:T(8,128)(2,1)S(1)} %collective-permute-done.la_ref, bf16[16,16,512]{2,1,0:T(8,128)(2,1)S(1)} %collective-permute-done.1.lb_ref, ...), custom_call_target="tpu_custom_call" | custom-call | flops 1073741824 | bytes 5248000 | tf_op jit(solution)/shard_map/near_projection/pallas_call | solution.py:339
  78.0 0.5 collective-permute-done.5.far_b_ref
  78.5 3.1 %collective-permute-done.4.far_a_ref = bf16[16,16,512]{2,1,0:T(8,128)(2,1)S(1)} collective-permute-done((bf16[16,16,512]{2,1,0:T(8,128)(2,1)S(1)}, bf16[16,16,512]{2,1,0:T(8,128)(2,1)S(1)}, u32[]{:S(2)}, u32[]{:S(2)}) %collective-permute-start.4) | collective-permute-done | bytes 262176 | tf_op jit(solution)/shard_map/ppermute | solution.py:469
  81.6 6.9 %coarse_layer.1 = (bf16[32,16,512]{2,1,0:T(8,128)(2,1)}, bf16[32,16,512]{2,1,0:T(8,128)(2,1)S(1)}) custom-call(s32[4,32]{1,0:T(4,128)S(1)} %reshape.60.table, s32[64]{0:T(128)S(1)} %reshape.62.blocks, s32[8]{0:T(128)S(1)} %get-tuple-element.40.counts, bf16[512,512]{1,0:T(8,128)(2,1)S(1)} %get-tuple-element.42.pooled_ref, ...), custom_call_target="tpu_custom_call" | custom-call | flops 4000000000 | bytes 13637184 | tf_op jit(solution)/shard_map/coarse_layer/pallas_call | solution.py:339
  88.6 16.5 %all_to_all.21.coarse_ref = bf16[32,16,512]{2,1,0:T(8,128)(2,1)S(1)} all-to-all(bf16[32,16,512]{2,1,0:T(8,128)(2,1)S(1)} %get-tuple-element.46), channel_id=1, replica_groups=mesh['pts'=32,'grp'=4] {'pts'}, dimensions={0} | all-to-all | bytes 1048576 | tf_op jit(solution)/shard_map/all_to_all | solution.py:356
  105.0 7.6 %third_layer.1 = bf16[32,64,256]{2,1,0:T(8,128)(2,1)S(1)} custom-call(s32[32]{0:T(128)S(1)} %select_reduce_fusion.place, bf16[8,256,256]{2,1,0:T(8,128)(2,1)S(1)} %get-tuple-element.38.x_ref, bf16[32,16,512]{2,1,0:T(8,128)(2,1)S(1)} %all_to_all.21.coarse_ref, f32[3,256]{1,0:T(4,128)S(1)} %copy-done.4, bf16[256,768]{1,0:T(8,128)(2,1)S(1)} %get-tuple-element.47.wqkv_ref, ...), custom_call_target="tpu_custom_call" | custom-call | flops 5000000000 | bytes 6297856 | tf_op jit(solution)/shard_map/third_layer/pallas_call | solution.py:339
  112.7 20.7 %all_to_all.22.x_ref = bf16[32,64,256]{2,1,0:T(8,128)(2,1)S(1)} all-to-all(bf16[32,64,256]{2,1,0:T(8,128)(2,1)S(1)} %third_layer.1), channel_id=1, replica_groups=mesh['pts'=32,'grp'=4] {'pts'}, dimensions={0} | all-to-all | bytes 2097152 | tf_op jit(solution)/shard_map/all_to_all | solution.py:356
  133.4 1.5 %ordered.1 = bf16[32,64,256]{2,1,0:T(8,128)(2,1)} custom-call(s32[4,32]{1,0:T(4,128)S(1)} %reshape.60.table, bf16[32,64,256]{2,1,0:T(8,128)(2,1)S(1)} %all_to_all.22.x_ref), custom_call_target="tpu_custom_call" | custom-call | bytes 2098176 | tf_op jit(solution)/shard_map/ordered/pallas_call | solution.py:339
  (12 shorter events, 0.1 us)
Async XLA Ops:
  9.3 9.7 %copy-start.7 = (s32[4096]{0:T(1024)S(1)}, s32[4096]{0:T(1024)}, u32[]{:S(2)}) copy-start(s32[4096]{0:T(1024)} %rot_hbm.1) | copy-start | bytes 49156
  9.3 9.9 %copy-start.9 = (s32[1,8]{1,0:T(1,128)S(1)}, s32[1,8]{1,0:T(1,128)}, u32[]{:S(2)}) copy-start(s32[1,8]{1,0:T(1,128)} %param.15) | copy-start | bytes 100
  9.3 10.1 %copy-start.8 = (s32[1,32]{1,0:T(1,128)S(1)}, s32[1,32]{1,0:T(1,128)}, u32[]{:S(2)}) copy-start(s32[1,32]{1,0:T(1,128)} %param.14) | copy-start | bytes 388
  9.3 11.6 %copy-start.6 = (bf16[3,256,256]{2,1,0:T(8,128)(2,1)S(1)}, bf16[3,256,256]{2,1,0:T(8,128)(2,1)}, u32[]{:S(2)}) copy-start(bf16[3,256,256]{2,1,0:T(8,128)(2,1)} %wo_hbm.1) | copy-start | bytes 1179652
  9.4 26.6 %all-to-all-start = ((bf16[32,64,256]{2,1,0:T(8,128)(2,1)}), bf16[32,64,256]{2,1,0:T(8,128)(2,1)S(1)}, u32[]{:S(2)}, u32[]{:S(2)}) async-start(bf16[32,64,256]{2,1,0:T(8,128)(2,1)} %first_layer.1), calls=%async_computation | async-start | bytes 2097152 | tf_op jit(solution)/shard_map/all_to_all | solution.py:356
  18.9 17.1 %copy-start.1 = (bf16[1024,512]{1,0:T(8,128)(2,1)S(1)}, bf16[1024,512]{1,0:T(8,128)(2,1)}, u32[]{:S(2)}) copy-start(bf16[1024,512]{1,0:T(8,128)(2,1)} %pool_ref.1) | copy-start | bytes 3145732
  18.9 17.0 %copy-start.4 = (f32[3,256]{1,0:T(4,128)S(1)}, f32[3,256]{1,0:T(4,128)}, u32[]{:S(2)}) copy-start(f32[3,256]{1,0:T(4,128)} %gain_ref.1) | copy-start | bytes 9220
  44.0 26.7 %copy-start = (bf16[512,1536]{1,0:T(8,128)(2,1)S(1)}, bf16[512,1536]{1,0:T(8,128)(2,1)}, u32[]{:S(2)}) copy-start(bf16[512,1536]{1,0:T(8,128)(2,1)} %w_ref.5) | copy-start | bytes 4718596
  44.0 26.7 %copy-start.5 = (f32[512]{0:T(512)S(1)}, f32[512]{0:T(512)}, u32[]{:S(2)}) copy-start(f32[512]{0:T(512)} %param.20) | copy-start | bytes 6148
  59.2 8.1 %collective-permute-start.3 = (bf16[16,16,512]{2,1,0:T(8,128)(2,1)S(1)}, bf16[16,16,512]{2,1,0:T(8,128)(2,1)S(1)}, u32[]{:S(2)}, u32[]{:S(2)}) collective-permute-start(bf16[16,16,512]{2,1,0:T(8,128)(2,1)S(1)} %get-tuple-element.54), channel_id=1, source_target_pairs={{0,3},{1,0},{2,1},{3,2},{4,7},{5,4},{6,5},{7,6},{8,11},{9,8},{10,9... | collective-permute-start | bytes 786440 | tf_op jit(solution)/shard_map/ppermute | solution.py:457
  62.0 8.7 %collective-permute-start = (bf16[16,16,512]{2,1,0:T(8,128)(2,1)S(1)}, bf16[16,16,512]{2,1,0:T(8,128)(2,1)S(1)}, u32[]{:S(2)}, u32[]{:S(2)}) collective-permute-start(bf16[16,16,512]{2,1,0:T(8,128)(2,1)S(1)} %get-tuple-element.55), channel_id=1, source_target_pairs={{0,1},{1,2},{2,3},{3,0},{4,5},{5,6},{6,7},{7,4},{8,9},{9,10},{10,1... | collective-permute-start | bytes 786440 | tf_op jit(solution)/shard_map/ppermute | solution.py:456
  62.0 14.0 %collective-permute-start.1 = (bf16[16,16,512]{2,1,0:T(8,128)(2,1)S(1)}, bf16[16,16,512]{2,1,0:T(8,128)(2,1)S(1)}, u32[]{:S(2)}, u32[]{:S(2)}) collective-permute-start(bf16[16,16,512]{2,1,0:T(8,128)(2,1)S(1)} %get-tuple-element.54), channel_id=1, source_target_pairs={{0,1},{1,2},{2,3},{3,0},{4,5},{5,6},{6,7},{7,4},{8,9},{9,10},{10,1... | collective-permute-start | bytes 786440 | tf_op jit(solution)/shard_map/ppermute | solution.py:458
  62.0 14.0 %collective-permute-start.2 = (bf16[16,16,512]{2,1,0:T(8,128)(2,1)S(1)}, bf16[16,16,512]{2,1,0:T(8,128)(2,1)S(1)}, u32[]{:S(2)}, u32[]{:S(2)}) collective-permute-start(bf16[16,16,512]{2,1,0:T(8,128)(2,1)S(1)} %get-tuple-element.55), channel_id=1, source_target_pairs={{0,3},{1,0},{2,1},{3,2},{4,7},{5,4},{6,5},{7,6},{8,11},{9,8},{10,9... | collective-permute-start | bytes 786440 | tf_op jit(solution)/shard_map/ppermute | solution.py:459
  67.3 11.2 %collective-permute-start.5 = (bf16[16,16,512]{2,1,0:T(8,128)(2,1)S(1)}, bf16[16,16,512]{2,1,0:T(8,128)(2,1)S(1)}, u32[]{:S(2)}, u32[]{:S(2)}) collective-permute-start(bf16[16,16,512]{2,1,0:T(8,128)(2,1)S(1)} %collective-permute-done.3.rb_ref), channel_id=1, source_target_pairs={{0,3},{1,0},{2,1},{3,2},{4,7},{5,4},{6,5},{7,6},{8,11},{9,8},{10,9... | collective-permute-start | bytes 786440 | tf_op jit(solution)/shard_map/ppermute | solution.py:470
  70.7 11.0 %collective-permute-start.4 = (bf16[16,16,512]{2,1,0:T(8,128)(2,1)S(1)}, bf16[16,16,512]{2,1,0:T(8,128)(2,1)S(1)}, u32[]{:S(2)}, u32[]{:S(2)}) collective-permute-start(bf16[16,16,512]{2,1,0:T(8,128)(2,1)S(1)} %collective-permute-done.la_ref), channel_id=1, source_target_pairs={{0,1},{1,2},{2,3},{3,0},{4,5},{5,6},{6,7},{7,4},{8,9},{9,10},{10,1... | collective-permute-start | bytes 786440 | tf_op jit(solution)/shard_map/ppermute | solution.py:469
  72.4 9.3 %copy-start.3 = (bf16[512,512]{1,0:T(8,128)(2,1)S(1)}, bf16[512,512]{1,0:T(8,128)(2,1)}, u32[]{:S(2)}) copy-start(bf16[512,512]{1,0:T(8,128)(2,1)} %wo_ref.1) | copy-start | bytes 1572868
  81.6 23.4 %copy-start.2 = (bf16[512,1024]{1,0:T(8,128)(2,1)S(1)}, bf16[512,1024]{1,0:T(8,128)(2,1)}, u32[]{:S(2)}) copy-start(bf16[512,1024]{1,0:T(8,128)(2,1)} %unpool_ref.1) | copy-start | bytes 3145732

commit v4 on v3

--- a/solution.py
+++ b/solution.py
@@ -35,11 +35,6 @@
     return (x * lax.rsqrt(jnp.mean(x * x, axis=-1, keepdims=True) + 1e-6) * gain).astype(BF16)
 
 
-def head_masks():
-    lane = lax.broadcasted_iota(jnp.int32, (1, 128), 1) // 32
-    return [(lane == i).astype(F32).astype(BF16) for i in range(4)]
-
-
 SCALE = LOG2E / math.sqrt(32.0)
 BALLS = SUBS // 4
 VM = pltpu.VMEM
@@ -54,7 +49,6 @@
 def fine_layer(load, reload, store, send, gain, wqvt_ref, wk_ref, wo_ref, scores, bufs, ready=None):
     left, right = scores
     k_s, qt_s, vt_s, ot_s = bufs[0:2], bufs[2:4], bufs[4:6], bufs[6:8]
-    masks = head_masks()
     ones = jnp.ones((16, BALL), BF16)
 
     def project(b, par):
@@ -65,8 +59,10 @@
         k_s[par][...] = dot(h, wk_ref[...]).astype(BF16)
 
     def score(dst, par, g, i):
-        keys = k_s[par][:, 128 * g : 128 * g + 128] * masks[i]
-        dst[BALL * i : BALL * (i + 1)] = dot(keys, qt_s[par][128 * g : 128 * g + 128, :])
+        at = 32 * (4 * g + i)
+        parts = [jnp.zeros((32 * i, BALL), BF16), qt_s[par][at : at + 32], jnp.zeros((96 - 32 * i, BALL), BF16)]
+        query = jnp.concatenate([p for p in parts if p.shape[0]], axis=0)
+        dst[BALL * i : BALL * (i + 1)] = dot(k_s[par][:, 128 * g : 128 * g + 128], query)
 
     def soft(src, par, g, i):
         s = src[BALL * i : BALL * (i + 1)]
@@ -78,43 +74,32 @@
     def finish(b, par):
         store(b, (reload(b) + dot(ot_s[par][...], wo_ref[...], TN)).astype(BF16))
 
-    ot_s[1][...] = jnp.zeros_like(ot_s[1])
     project(0, 0)
     for i in range(4):
         score(left, 0, 0, i)
     if ready is not None:
         ready()
-
-    def step(b, par):
-        project(jnp.minimum(b + 1, BALLS - 1), 1 - par)
+    for b in range(BALLS):
+        par, last = b % 2, b == BALLS - 1
+        if send is not None and b % 2 == 0:
+            for done in (b - 3, b - 2):
+                if done >= 0:
+                    send(done)
+        if not last:
+            project(b + 1, 1 - par)
         for i in range(4):
             score(right, par, 1, i)
             soft(left, par, 0, i)
-        finish(jnp.maximum(b - 1, 0), 1 - par)
+        if b > 0:
+            finish(b - 1, 1 - par)
         for i in range(4):
-            score(left, 1 - par, 0, i)
+            if not last:
+                score(left, 1 - par, 0, i)
             soft(right, par, 1, i)
-
-    def pair(t, carry):
-        if send is not None:
-
-            @pl.when(t >= 1)
-            def _():
-                send(2 * t - 2)
-
-            @pl.when(t >= 2)
-            def _():
-                send(2 * t - 3)
-
-        step(2 * t, 0)
-        step(2 * t + 1, 1)
-        return carry
-
-    lax.fori_loop(0, BALLS // 2, pair, 0)
     if send is not None:
         send(BALLS - 3)
         send(BALLS - 2)
-    finish(BALLS - 1, 1)
+    finish(BALLS - 1, (BALLS - 1) % 2)
     if send is not None:
         send(BALLS - 1)
 
@@ -320,7 +305,7 @@
         soft(b_ref, b, 1)
         return carry
 
-    lax.fori_loop(0, count, block, 0, unroll=2)
+    lax.fori_loop(0, count, block, 0, unroll=8)
     part = SUBS // 4
     for c in range(4):
         at = slice(part * POOL * c, part * POOL * (c + 1))

time: 135 us -> 132 us (0.978)
  Pallas kernels: 36.4 us -> 32.9 us
    pallas_call x7, Pallas kernels: 36.4 us -> 32.9 us  [call(): pl.pallas_call(kernel, out_shape=outs, in_specs=specs or [SMEM] * tables...]
where the time goes in v4:
time: 132 us
  blocking collectives  52.3 us (40%)
  Pallas kernels  32.9 us (25%)
  waiting for transfers between devices  23.7 us (18%)
  starting transfers between devices  18.5 us (14%)
  other arithmetic  1.64 us (1%)
  local copies, waits for them, and re-layouts  1.54 us (1%)
    all_to_all x3, blocking collectives, exchange(): lax.all_to_all(pieces, 'pts', split_axis=0, concat_axis=0, tiled=True)  52.3 us
    pallas_call x7, Pallas kernels, call(): pl.pallas_call(kernel, out_shape=outs, in_specs=specs or [SMEM] * tables...  32.9 us
    all_to_all x1, waiting for transfers between devices, exchange(): lax.all_to_all(pieces, 'pts', split_axis=0, concat_axis=0, tiled=True)  13.9 us
    all_to_all x1, starting transfers between devices, exchange(): lax.all_to_all(pieces, 'pts', split_axis=0, concat_axis=0, tiled=True)  9.58 us
    ppermute x1, waiting for transfers between devices, body(): left_b = lax.ppermute(pieces[half:], 'grp', up)  3.65 us
    ppermute x1, starting transfers between devices, body(): far_b = lax.ppermute(right_b, 'grp', down)  3.41 us
    ppermute x1, waiting for transfers between devices, body(): far_a = lax.ppermute(left_a, 'grp', up)  3.13 us
    ppermute x1, starting transfers between devices, body(): right_b = lax.ppermute(pieces[half:], 'grp', down)  2.8 us
  transfers between devices with their start and end apart: 7, of which 5 were waited for; matrix products, arithmetic and copies ran while one was open for 2% of the time, Pallas kernels for 3%

profile of v4, /device:TPU:1, one launch (start us, length us, event | category | flops | bytes accessed | tf_op | source)
XLA Modules:
  0.0 131.7 jit_solution(12528990487590058407)
XLA Ops:
  0.6 8.0 %first_layer.1 = bf16[32,64,256]{2,1,0:T(8,128)(2,1)} custom-call(s32[4096]{0:T(1024)} %rot_hbm.1, f32[3,256]{1,0:T(4,128)} %gain_ref.1, bf16[32,64,256]{2,1,0:T(8,128)(2,1)} %bitcast.30, bf16[3,256,768]{2,1,0:T(8,128)(2,1)} %wqkv_hbm.1, bf16[3,256,256]{2,1,0:T(8,128)(2,1)} %wo_hbm.1), custom_call_target="tpu_custom_call" | custom-call | flops 5000000000 | bytes 5281792 | tf_op jit(solution)/shard_map/first_layer/pallas_call | solution.py:324
  8.6 0.0 copy-start.7
  8.6 0.0 copy-start.9
  8.6 0.0 copy-start.8
  8.6 0.0 copy-start.6
  8.7 9.6 %all-to-all-start = ((bf16[32,64,256]{2,1,0:T(8,128)(2,1)}), bf16[32,64,256]{2,1,0:T(8,128)(2,1)S(1)}, u32[]{:S(2)}, u32[]{:S(2)}) async-start(bf16[32,64,256]{2,1,0:T(8,128)(2,1)} %first_layer.1), calls=%async_computation | async-start | bytes 2097152 | tf_op jit(solution)/shard_map/all_to_all | solution.py:341
  18.2 0.0 copy-start.1
  18.2 0.0 copy-start.4
  18.3 0.0 copy-done.7
  18.3 0.1 reshape.61
  18.4 0.1 and_select_fusion
  18.5 0.0 copy-done.9
  18.5 0.1 select_reduce_fusion.5
  18.6 0.1 reshape.60.table
  18.7 0.2 select_reduce_fusion.4
  18.9 0.2 select_reduce_fusion.2
  19.1 0.1 add_minimum_fusion
  19.1 0.3 select_reduce_fusion.1
  19.4 0.1 reshape.62.blocks
  19.5 0.7 select_reduce_fusion.place
  20.3 1.2 slice_bitcast_fusion
  21.4 13.9 %all-to-all-done.x_ref = bf16[32,64,256]{2,1,0:T(8,128)(2,1)S(1)} async-done(((bf16[32,64,256]{2,1,0:T(8,128)(2,1)}), bf16[32,64,256]{2,1,0:T(8,128)(2,1)S(1)}, u32[]{:S(2)}, u32[]{:S(2)}) %all-to-all-start) | async-done | bytes 1048608 | tf_op jit(solution)/shard_map/all_to_all | solution.py:341
  35.3 0.0 copy-done.4
  35.3 6.9 %second_layer.1 = (bf16[8,256,256]{2,1,0:T(8,128)(2,1)S(1)}, bf16[32,16,512]{2,1,0:T(8,128)(2,1)S(1)}) custom-call(s32[32]{0:T(128)S(1)} %select_reduce_fusion.place, bf16[32,64,256]{2,1,0:T(8,128)(2,1)S(1)} %all-to-all-done.x_ref, f32[3,256]{1,0:T(4,128)S(1)} %copy-done.4, bf16[256,768]{1,0:T(8,128)(2,1)S(1)} %get-tuple-element.36.wqkv_ref, ...), custom_call_target="tpu_custom_call" | custom-call | flops 5000000000 | bytes 5249280 | tf_op jit(solution)/shard_map/second_layer/pallas_call | solution.py:324
  42.2 0.0 copy-start
  42.2 0.0 copy-start.5
  42.2 15.2 %all_to_all.20.pieces_ref = bf16[32,16,512]{2,1,0:T(8,128)(2,1)S(1)} all-to-all(bf16[32,16,512]{2,1,0:T(8,128)(2,1)S(1)} %get-tuple-element.41), channel_id=1, replica_groups=mesh['pts'=32,'grp'=4] {'pts'}, dimensions={0} | all-to-all | bytes 1048576 | tf_op jit(solution)/shard_map/all_to_all | solution.py:341
  57.4 2.8 %collective-permute-start.3 = (bf16[16,16,512]{2,1,0:T(8,128)(2,1)S(1)}, bf16[16,16,512]{2,1,0:T(8,128)(2,1)S(1)}, u32[]{:S(2)}, u32[]{:S(2)}) collective-permute-start(bf16[16,16,512]{2,1,0:T(8,128)(2,1)S(1)} %get-tuple-element.54), channel_id=1, source_target_pairs={{0,3},{1,0},{2,1},{3,2},{4,7},{5,4},{6,5},{7,6},{8,11},{9,8},{10,9... | collective-permute-start | bytes 786440 | tf_op jit(solution)/shard_map/ppermute | solution.py:442
  60.2 0.0 collective-permute-start
  60.2 0.0 collective-permute-start.1
  60.3 2.7 %collective-permute-start.2 = (bf16[16,16,512]{2,1,0:T(8,128)(2,1)S(1)}, bf16[16,16,512]{2,1,0:T(8,128)(2,1)S(1)}, u32[]{:S(2)}, u32[]{:S(2)}) collective-permute-start(bf16[16,16,512]{2,1,0:T(8,128)(2,1)S(1)} %get-tuple-element.55), channel_id=1, source_target_pairs={{0,3},{1,0},{2,1},{3,2},{4,7},{5,4},{6,5},{7,6},{8,11},{9,8},{10,9... | collective-permute-start | bytes 786440 | tf_op jit(solution)/shard_map/ppermute | solution.py:444
  62.9 2.6 %collective-permute-done.3.rb_ref = bf16[16,16,512]{2,1,0:T(8,128)(2,1)S(1)} collective-permute-done((bf16[16,16,512]{2,1,0:T(8,128)(2,1)S(1)}, bf16[16,16,512]{2,1,0:T(8,128)(2,1)S(1)}, u32[]{:S(2)}, u32[]{:S(2)}) %collective-permute-start.3) | collective-permute-done | bytes 262176 | tf_op jit(solution)/shard_map/ppermute | solution.py:442
  65.5 3.4 %collective-permute-start.5 = (bf16[16,16,512]{2,1,0:T(8,128)(2,1)S(1)}, bf16[16,16,512]{2,1,0:T(8,128)(2,1)S(1)}, u32[]{:S(2)}, u32[]{:S(2)}) collective-permute-start(bf16[16,16,512]{2,1,0:T(8,128)(2,1)S(1)} %collective-permute-done.3.rb_ref), channel_id=1, source_target_pairs={{0,3},{1,0},{2,1},{3,2},{4,7},{5,4},{6,5},{7,6},{8,11},{9,8},{10,9... | collective-permute-start | bytes 786440 | tf_op jit(solution)/shard_map/ppermute | solution.py:455
  68.9 0.0 collective-permute-done.la_ref
  68.9 0.0 collective-permute-start.4
  68.9 1.6 %own_projection.1 = (bf16[512,512]{1,0:T(8,128)(2,1)S(1)}, bf16[512,1536]{1,0:T(8,128)(2,1)S(1)}) custom-call(s32[4,32]{1,0:T(4,128)S(1)} %reshape.60.table, bf16[32,16,512]{2,1,0:T(8,128)(2,1)S(1)} %all_to_all.20.pieces_ref, f32[1,512]{1,0:T(1,128)S(1)} %bitcast.21, bf16[512,1536]{1,0:T(8,128)(2,1)S(1)} %copy-done), custom_call_target="tpu_custom_call" | custom-call | flops 805306368 | bytes 4199424 | tf_op jit(solution)/shard_map/own_projection/pallas_call | solution.py:324
  70.6 0.0 copy-start.3
  70.6 3.6 %collective-permute-done.1.lb_ref = bf16[16,16,512]{2,1,0:T(8,128)(2,1)S(1)} collective-permute-done((bf16[16,16,512]{2,1,0:T(8,128)(2,1)S(1)}, bf16[16,16,512]{2,1,0:T(8,128)(2,1)S(1)}, u32[]{:S(2)}, u32[]{:S(2)}) %collective-permute-start.1) | collective-permute-done | bytes 262176 | tf_op jit(solution)/shard_map/ppermute | solution.py:443
  74.2 0.0 collective-permute-done.2.ra_ref
  74.2 2.0 %near_projection.1 = (bf16[512,1024]{1,0:T(8,128)(2,1)S(1)}, bf16[512,1024]{1,0:T(8,128)(2,1)S(1)}) custom-call(s32[4,32]{1,0:T(4,128)S(1)} %reshape.60.table, bf16[16,16,512]{2,1,0:T(8,128)(2,1)S(1)} %collective-permute-done.la_ref, bf16[16,16,512]{2,1,0:T(8,128)(2,1)S(1)} %collective-permute-done.1.lb_ref, ...), custom_call_target="tpu_custom_call" | custom-call | flops 1073741824 | bytes 5248000 | tf_op jit(solution)/shard_map/near_projection/pallas_call | solution.py:324
  76.2 0.5 collective-permute-done.5.far_b_ref
  76.7 3.1 %collective-permute-done.4.far_a_ref = bf16[16,16,512]{2,1,0:T(8,128)(2,1)S(1)} collective-permute-done((bf16[16,16,512]{2,1,0:T(8,128)(2,1)S(1)}, bf16[16,16,512]{2,1,0:T(8,128)(2,1)S(1)}, u32[]{:S(2)}, u32[]{:S(2)}) %collective-permute-start.4) | collective-permute-done | bytes 262176 | tf_op jit(solution)/shard_map/ppermute | solution.py:454
  79.9 6.2 %coarse_layer.1 = (bf16[32,16,512]{2,1,0:T(8,128)(2,1)}, bf16[32,16,512]{2,1,0:T(8,128)(2,1)S(1)}) custom-call(s32[4,32]{1,0:T(4,128)S(1)} %reshape.60.table, s32[64]{0:T(128)S(1)} %reshape.62.blocks, s32[8]{0:T(128)S(1)} %get-tuple-element.40.counts, bf16[512,512]{1,0:T(8,128)(2,1)S(1)} %get-tuple-element.42.pooled_ref, ...), custom_call_target="tpu_custom_call" | custom-call | flops 4000000000 | bytes 13637184 | tf_op jit(solution)/shard_map/coarse_layer/pallas_call | solution.py:324
  86.0 16.5 %all_to_all.21.coarse_ref = bf16[32,16,512]{2,1,0:T(8,128)(2,1)S(1)} all-to-all(bf16[32,16,512]{2,1,0:T(8,128)(2,1)S(1)} %get-tuple-element.46), channel_id=1, replica_groups=mesh['pts'=32,'grp'=4] {'pts'}, dimensions={0} | all-to-all | bytes 1048576 | tf_op jit(solution)/shard_map/all_to_all | solution.py:341
  102.5 0.0 copy-done.2
  102.5 6.7 %third_layer.1 = bf16[32,64,256]{2,1,0:T(8,128)(2,1)S(1)} custom-call(s32[32]{0:T(128)S(1)} %select_reduce_fusion.place, bf16[8,256,256]{2,1,0:T(8,128)(2,1)S(1)} %get-tuple-element.38.x_ref, bf16[32,16,512]{2,1,0:T(8,128)(2,1)S(1)} %all_to_all.21.coarse_ref, f32[3,256]{1,0:T(4,128)S(1)} %copy-done.4, bf16[256,768]{1,0:T(8,128)(2,1)S(1)} %get-tuple-element.47.wqkv_ref, ...), custom_call_target="tpu_custom_call" | custom-call | flops 5000000000 | bytes 6297856 | tf_op jit(solution)/shard_map/third_layer/pallas_call | solution.py:324
  109.2 20.7 %all_to_all.22.x_ref = bf16[32,64,256]{2,1,0:T(8,128)(2,1)S(1)} all-to-all(bf16[32,64,256]{2,1,0:T(8,128)(2,1)S(1)} %third_layer.1), channel_id=1, replica_groups=mesh['pts'=32,'grp'=4] {'pts'}, dimensions={0} | all-to-all | bytes 2097152 | tf_op jit(solution)/shard_map/all_to_all | solution.py:341
  129.9 1.5 %ordered.1 = bf16[32,64,256]{2,1,0:T(8,128)(2,1)} custom-call(s32[4,32]{1,0:T(4,128)S(1)} %reshape.60.table, bf16[32,64,256]{2,1,0:T(8,128)(2,1)S(1)} %all_to_all.22.x_ref), custom_call_target="tpu_custom_call" | custom-call | bytes 2098176 | tf_op jit(solution)/shard_map/ordered/pallas_call | solution.py:324
  (12 shorter events, 0.1 us)
Async XLA Ops:
  8.6 9.7 %copy-start.7 = (s32[4096]{0:T(1024)S(1)}, s32[4096]{0:T(1024)}, u32[]{:S(2)}) copy-start(s32[4096]{0:T(1024)} %rot_hbm.1) | copy-start | bytes 49156
  8.6 9.9 %copy-start.9 = (s32[1,8]{1,0:T(1,128)S(1)}, s32[1,8]{1,0:T(1,128)}, u32[]{:S(2)}) copy-start(s32[1,8]{1,0:T(1,128)} %param.15) | copy-start | bytes 100
  8.6 10.1 %copy-start.8 = (s32[1,32]{1,0:T(1,128)S(1)}, s32[1,32]{1,0:T(1,128)}, u32[]{:S(2)}) copy-start(s32[1,32]{1,0:T(1,128)} %param.14) | copy-start | bytes 388
  8.6 11.6 %copy-start.6 = (bf16[3,256,256]{2,1,0:T(8,128)(2,1)S(1)}, bf16[3,256,256]{2,1,0:T(8,128)(2,1)}, u32[]{:S(2)}) copy-start(bf16[3,256,256]{2,1,0:T(8,128)(2,1)} %wo_hbm.1) | copy-start | bytes 1179652
  8.7 26.6 %all-to-all-start = ((bf16[32,64,256]{2,1,0:T(8,128)(2,1)}), bf16[32,64,256]{2,1,0:T(8,128)(2,1)S(1)}, u32[]{:S(2)}, u32[]{:S(2)}) async-start(bf16[32,64,256]{2,1,0:T(8,128)(2,1)} %first_layer.1), calls=%async_computation | async-start | bytes 2097152 | tf_op jit(solution)/shard_map/all_to_all | solution.py:341
  18.2 17.0 %copy-start.1 = (bf16[1024,512]{1,0:T(8,128)(2,1)S(1)}, bf16[1024,512]{1,0:T(8,128)(2,1)}, u32[]{:S(2)}) copy-start(bf16[1024,512]{1,0:T(8,128)(2,1)} %pool_ref.1) | copy-start | bytes 3145732
  18.2 17.0 %copy-start.4 = (f32[3,256]{1,0:T(4,128)S(1)}, f32[3,256]{1,0:T(4,128)}, u32[]{:S(2)}) copy-start(f32[3,256]{1,0:T(4,128)} %gain_ref.1) | copy-start | bytes 9220
  42.2 26.7 %copy-start = (bf16[512,1536]{1,0:T(8,128)(2,1)S(1)}, bf16[512,1536]{1,0:T(8,128)(2,1)}, u32[]{:S(2)}) copy-start(bf16[512,1536]{1,0:T(8,128)(2,1)} %w_ref.5) | copy-start | bytes 4718596
  42.2 26.7 %copy-start.5 = (f32[512]{0:T(512)S(1)}, f32[512]{0:T(512)}, u32[]{:S(2)}) copy-start(f32[512]{0:T(512)} %param.20) | copy-start | bytes 6148
  57.4 8.1 %collective-permute-start.3 = (bf16[16,16,512]{2,1,0:T(8,128)(2,1)S(1)}, bf16[16,16,512]{2,1,0:T(8,128)(2,1)S(1)}, u32[]{:S(2)}, u32[]{:S(2)}) collective-permute-start(bf16[16,16,512]{2,1,0:T(8,128)(2,1)S(1)} %get-tuple-element.54), channel_id=1, source_target_pairs={{0,3},{1,0},{2,1},{3,2},{4,7},{5,4},{6,5},{7,6},{8,11},{9,8},{10,9... | collective-permute-start | bytes 786440 | tf_op jit(solution)/shard_map/ppermute | solution.py:442
  60.2 8.7 %collective-permute-start = (bf16[16,16,512]{2,1,0:T(8,128)(2,1)S(1)}, bf16[16,16,512]{2,1,0:T(8,128)(2,1)S(1)}, u32[]{:S(2)}, u32[]{:S(2)}) collective-permute-start(bf16[16,16,512]{2,1,0:T(8,128)(2,1)S(1)} %get-tuple-element.55), channel_id=1, source_target_pairs={{0,1},{1,2},{2,3},{3,0},{4,5},{5,6},{6,7},{7,4},{8,9},{9,10},{10,1... | collective-permute-start | bytes 786440 | tf_op jit(solution)/shard_map/ppermute | solution.py:441
  60.2 14.0 %collective-permute-start.1 = (bf16[16,16,512]{2,1,0:T(8,128)(2,1)S(1)}, bf16[16,16,512]{2,1,0:T(8,128)(2,1)S(1)}, u32[]{:S(2)}, u32[]{:S(2)}) collective-permute-start(bf16[16,16,512]{2,1,0:T(8,128)(2,1)S(1)} %get-tuple-element.54), channel_id=1, source_target_pairs={{0,1},{1,2},{2,3},{3,0},{4,5},{5,6},{6,7},{7,4},{8,9},{9,10},{10,1... | collective-permute-start | bytes 786440 | tf_op jit(solution)/shard_map/ppermute | solution.py:443
  60.3 14.0 %collective-permute-start.2 = (bf16[16,16,512]{2,1,0:T(8,128)(2,1)S(1)}, bf16[16,16,512]{2,1,0:T(8,128)(2,1)S(1)}, u32[]{:S(2)}, u32[]{:S(2)}) collective-permute-start(bf16[16,16,512]{2,1,0:T(8,128)(2,1)S(1)} %get-tuple-element.55), channel_id=1, source_target_pairs={{0,3},{1,0},{2,1},{3,2},{4,7},{5,4},{6,5},{7,6},{8,11},{9,8},{10,9... | collective-permute-start | bytes 786440 | tf_op jit(solution)/shard_map/ppermute | solution.py:444
  65.5 11.2 %collective-permute-start.5 = (bf16[16,16,512]{2,1,0:T(8,128)(2,1)S(1)}, bf16[16,16,512]{2,1,0:T(8,128)(2,1)S(1)}, u32[]{:S(2)}, u32[]{:S(2)}) collective-permute-start(bf16[16,16,512]{2,1,0:T(8,128)(2,1)S(1)} %collective-permute-done.3.rb_ref), channel_id=1, source_target_pairs={{0,3},{1,0},{2,1},{3,2},{4,7},{5,4},{6,5},{7,6},{8,11},{9,8},{10,9... | collective-permute-start | bytes 786440 | tf_op jit(solution)/shard_map/ppermute | solution.py:455
  68.9 11.0 %collective-permute-start.4 = (bf16[16,16,512]{2,1,0:T(8,128)(2,1)S(1)}, bf16[16,16,512]{2,1,0:T(8,128)(2,1)S(1)}, u32[]{:S(2)}, u32[]{:S(2)}) collective-permute-start(bf16[16,16,512]{2,1,0:T(8,128)(2,1)S(1)} %collective-permute-done.la_ref), channel_id=1, source_target_pairs={{0,1},{1,2},{2,3},{3,0},{4,5},{5,6},{6,7},{7,4},{8,9},{9,10},{10,1... | collective-permute-start | bytes 786440 | tf_op jit(solution)/shard_map/ppermute | solution.py:454
  70.6 9.3 %copy-start.3 = (bf16[512,512]{1,0:T(8,128)(2,1)S(1)}, bf16[512,512]{1,0:T(8,128)(2,1)}, u32[]{:S(2)}) copy-start(bf16[512,512]{1,0:T(8,128)(2,1)} %wo_ref.1) | copy-start | bytes 1572868
  79.9 22.6 %copy-start.2 = (bf16[512,1024]{1,0:T(8,128)(2,1)S(1)}, bf16[512,1024]{1,0:T(8,128)(2,1)}, u32[]{:S(2)}) copy-start(bf16[512,1024]{1,0:T(8,128)(2,1)} %unpool_ref.1) | copy-start | bytes 3145732

commit v5 on v4

--- a/solution.py
+++ b/solution.py
@@ -121,7 +121,12 @@
 ):
     groups = lax.axis_size("grp")
     device = lax.axis_index("pts") * groups + lax.axis_index("grp")
-    weights = pltpu.make_async_copy(wqkv_hbm.at[0], wqkv_ref, sems.at[0])
+    query, key, value = [
+        pltpu.make_async_copy(
+            wqkv_hbm.at[0, :, pl.ds(WIDTH * c, WIDTH)], wqkv_ref.at[:, pl.ds(WIDTH * c, WIDTH)], sems.at[7 + c]
+        )
+        for c in range(3)
+    ]
     early = pltpu.make_async_copy(x_hbm.at[pl.ds(0, 4)], x_ref.at[pl.ds(0, 4)], sems.at[1])
     gains = pltpu.make_async_copy(gain_hbm, gain_ref, sems.at[2])
     late = [
@@ -129,15 +134,17 @@
         pltpu.make_async_copy(wo_hbm.at[0], wo_ref, sems.at[4]),
         pltpu.make_async_copy(rot_hbm, rot, sems.at[5]),
     ]
-    weights.start()
-    early.start()
-    gains.start()
-    weights.wait()
+    for copy in (query, value, early, gains, key):
+        copy.start()
+    query.wait()
+    wqvt_ref[:WIDTH] = wqkv_ref[:, :WIDTH].T
+    value.wait()
     for copy in late:
         copy.start()
-    transposed(wqkv_ref, wqvt_ref)
+    wqvt_ref[WIDTH:] = wqkv_ref[:, 2 * WIDTH :].T
     early.wait()
     gains.wait()
+    key.wait()
 
     def ready():
         for copy in late:
@@ -404,7 +411,7 @@
             VM((width, 3 * width), BF16),
             VM((width, width), BF16),
             VM((SUBS, SUB, width), BF16),
-            pltpu.SemaphoreType.DMA((7,)),
+            pltpu.SemaphoreType.DMA((10,)),
         ]
         + FINE_SCRATCH,
         (rot_dest, fine_gain, points.reshape(SUBS, SUB, width), fine_qkv, fine_out),

time: 132 us -> 132 us (level)
  no operation moved by 1% of the time
where the time goes in v5:
time: 132 us
  blocking collectives  52.3 us (40%)
  Pallas kernels  33 us (25%)
  waiting for transfers between devices  23.7 us (18%)
  starting transfers between devices  18.5 us (14%)
  other arithmetic  1.64 us (1%)
  local copies, waits for them, and re-layouts  1.54 us (1%)
    all_to_all x3, blocking collectives, exchange(): lax.all_to_all(pieces, 'pts', split_axis=0, concat_axis=0, tiled=True)  52.3 us
    pallas_call x7, Pallas kernels, call(): pl.pallas_call(kernel, out_shape=outs, in_specs=specs or [SMEM] * tables...  33 us
    all_to_all x1, waiting for transfers between devices, exchange(): lax.all_to_all(pieces, 'pts', split_axis=0, concat_axis=0, tiled=True)  13.9 us
    all_to_all x1, starting transfers between devices, exchange(): lax.all_to_all(pieces, 'pts', split_axis=0, concat_axis=0, tiled=True)  9.57 us
    ppermute x1, waiting for transfers between devices, body(): left_b = lax.ppermute(pieces[half:], 'grp', up)  3.65 us
    ppermute x1, starting transfers between devices, body(): far_b = lax.ppermute(right_b, 'grp', down)  3.41 us
    ppermute x1, waiting for transfers between devices, body(): far_a = lax.ppermute(left_a, 'grp', up)  3.13 us
    ppermute x1, starting transfers between devices, body(): right_b = lax.ppermute(pieces[half:], 'grp', down)  2.8 us
  transfers between devices with their start and end apart: 7, of which 5 were waited for; matrix products, arithmetic and copies ran while one was open for 2% of the time, Pallas kernels for 3%

profile of v5, /device:TPU:1, one launch (start us, length us, event | category | flops | bytes accessed | tf_op | source)
XLA Modules:
  0.0 131.7 jit_solution(928196986257267413)
XLA Ops:
  0.6 8.0 %first_layer.1 = bf16[32,64,256]{2,1,0:T(8,128)(2,1)} custom-call(s32[4096]{0:T(1024)} %rot_hbm.1, f32[3,256]{1,0:T(4,128)} %gain_ref.1, bf16[32,64,256]{2,1,0:T(8,128)(2,1)} %bitcast.30, bf16[3,256,768]{2,1,0:T(8,128)(2,1)} %wqkv_hbm.1, bf16[3,256,256]{2,1,0:T(8,128)(2,1)} %wo_hbm.1), custom_call_target="tpu_custom_call" | custom-call | flops 5000000000 | bytes 5281792 | tf_op jit(solution)/shard_map/first_layer/pallas_call | solution.py:331
  8.6 0.0 copy-start.7
  8.7 0.0 copy-start.9
  8.7 0.0 copy-start.8
  8.7 0.0 copy-start.6
  8.7 9.6 %all-to-all-start = ((bf16[32,64,256]{2,1,0:T(8,128)(2,1)}), bf16[32,64,256]{2,1,0:T(8,128)(2,1)S(1)}, u32[]{:S(2)}, u32[]{:S(2)}) async-start(bf16[32,64,256]{2,1,0:T(8,128)(2,1)} %first_layer.1), calls=%async_computation | async-start | bytes 2097152 | tf_op jit(solution)/shard_map/all_to_all | solution.py:348
  18.3 0.0 copy-start.1
  18.3 0.0 copy-start.4
  18.3 0.0 copy-done.7
  18.3 0.1 reshape.61
  18.4 0.1 and_select_fusion
  18.5 0.0 copy-done.9
  18.5 0.1 select_reduce_fusion.5
  18.7 0.1 reshape.60.table
  18.7 0.0 copy-done.8
  18.7 0.2 select_reduce_fusion.4
  18.9 0.2 select_reduce_fusion.2
  19.1 0.1 add_minimum_fusion
  19.2 0.3 select_reduce_fusion.1
  19.5 0.1 reshape.62.blocks
  19.6 0.7 select_reduce_fusion.place
  20.3 0.0 copy-done.6
  20.3 1.2 slice_bitcast_fusion
  21.5 13.9 %all-to-all-done.x_ref = bf16[32,64,256]{2,1,0:T(8,128)(2,1)S(1)} async-done(((bf16[32,64,256]{2,1,0:T(8,128)(2,1)}), bf16[32,64,256]{2,1,0:T(8,128)(2,1)S(1)}, u32[]{:S(2)}, u32[]{:S(2)}) %all-to-all-start) | async-done | bytes 1048608 | tf_op jit(solution)/shard_map/all_to_all | solution.py:348
  35.3 6.9 %second_layer.1 = (bf16[8,256,256]{2,1,0:T(8,128)(2,1)S(1)}, bf16[32,16,512]{2,1,0:T(8,128)(2,1)S(1)}) custom-call(s32[32]{0:T(128)S(1)} %select_reduce_fusion.place, bf16[32,64,256]{2,1,0:T(8,128)(2,1)S(1)} %all-to-all-done.x_ref, f32[3,256]{1,0:T(4,128)S(1)} %copy-done.4, bf16[256,768]{1,0:T(8,128)(2,1)S(1)} %get-tuple-element.36.wqkv_ref, ...), custom_call_target="tpu_custom_call" | custom-call | flops 5000000000 | bytes 5249280 | tf_op jit(solution)/shard_map/second_layer/pallas_call | solution.py:331
  42.2 0.0 copy-start
  42.2 0.0 copy-start.5
  42.3 15.2 %all_to_all.20.pieces_ref = bf16[32,16,512]{2,1,0:T(8,128)(2,1)S(1)} all-to-all(bf16[32,16,512]{2,1,0:T(8,128)(2,1)S(1)} %get-tuple-element.41), channel_id=1, replica_groups=mesh['pts'=32,'grp'=4] {'pts'}, dimensions={0} | all-to-all | bytes 1048576 | tf_op jit(solution)/shard_map/all_to_all | solution.py:348
  57.5 2.8 %collective-permute-start.3 = (bf16[16,16,512]{2,1,0:T(8,128)(2,1)S(1)}, bf16[16,16,512]{2,1,0:T(8,128)(2,1)S(1)}, u32[]{:S(2)}, u32[]{:S(2)}) collective-permute-start(bf16[16,16,512]{2,1,0:T(8,128)(2,1)S(1)} %get-tuple-element.54), channel_id=1, source_target_pairs={{0,3},{1,0},{2,1},{3,2},{4,7},{5,4},{6,5},{7,6},{8,11},{9,8},{10,9... | collective-permute-start | bytes 786440 | tf_op jit(solution)/shard_map/ppermute | solution.py:449
  60.3 0.0 collective-permute-start
  60.3 0.0 collective-permute-start.1
  60.3 2.7 %collective-permute-start.2 = (bf16[16,16,512]{2,1,0:T(8,128)(2,1)S(1)}, bf16[16,16,512]{2,1,0:T(8,128)(2,1)S(1)}, u32[]{:S(2)}, u32[]{:S(2)}) collective-permute-start(bf16[16,16,512]{2,1,0:T(8,128)(2,1)S(1)} %get-tuple-element.55), channel_id=1, source_target_pairs={{0,3},{1,0},{2,1},{3,2},{4,7},{5,4},{6,5},{7,6},{8,11},{9,8},{10,9... | collective-permute-start | bytes 786440 | tf_op jit(solution)/shard_map/ppermute | solution.py:451
  63.0 2.6 %collective-permute-done.3.rb_ref = bf16[16,16,512]{2,1,0:T(8,128)(2,1)S(1)} collective-permute-done((bf16[16,16,512]{2,1,0:T(8,128)(2,1)S(1)}, bf16[16,16,512]{2,1,0:T(8,128)(2,1)S(1)}, u32[]{:S(2)}, u32[]{:S(2)}) %collective-permute-start.3) | collective-permute-done | bytes 262176 | tf_op jit(solution)/shard_map/ppermute | solution.py:449
  65.5 3.4 %collective-permute-start.5 = (bf16[16,16,512]{2,1,0:T(8,128)(2,1)S(1)}, bf16[16,16,512]{2,1,0:T(8,128)(2,1)S(1)}, u32[]{:S(2)}, u32[]{:S(2)}) collective-permute-start(bf16[16,16,512]{2,1,0:T(8,128)(2,1)S(1)} %collective-permute-done.3.rb_ref), channel_id=1, source_target_pairs={{0,3},{1,0},{2,1},{3,2},{4,7},{5,4},{6,5},{7,6},{8,11},{9,8},{10,9... | collective-permute-start | bytes 786440 | tf_op jit(solution)/shard_map/ppermute | solution.py:462
  68.9 0.0 collective-permute-done.la_ref
  69.0 0.0 collective-permute-start.4
  69.0 1.6 %own_projection.1 = (bf16[512,512]{1,0:T(8,128)(2,1)S(1)}, bf16[512,1536]{1,0:T(8,128)(2,1)S(1)}) custom-call(s32[4,32]{1,0:T(4,128)S(1)} %reshape.60.table, bf16[32,16,512]{2,1,0:T(8,128)(2,1)S(1)} %all_to_all.20.pieces_ref, f32[1,512]{1,0:T(1,128)S(1)} %bitcast.21, bf16[512,1536]{1,0:T(8,128)(2,1)S(1)} %copy-done), custom_call_target="tpu_custom_call" | custom-call | flops 805306368 | bytes 4199424 | tf_op jit(solution)/shard_map/own_projection/pallas_call | solution.py:331
  70.6 0.0 copy-start.3
  70.6 3.6 %collective-permute-done.1.lb_ref = bf16[16,16,512]{2,1,0:T(8,128)(2,1)S(1)} collective-permute-done((bf16[16,16,512]{2,1,0:T(8,128)(2,1)S(1)}, bf16[16,16,512]{2,1,0:T(8,128)(2,1)S(1)}, u32[]{:S(2)}, u32[]{:S(2)}) %collective-permute-start.1) | collective-permute-done | bytes 262176 | tf_op jit(solution)/shard_map/ppermute | solution.py:450
  74.3 0.0 collective-permute-done.2.ra_ref
  74.3 2.0 %near_projection.1 = (bf16[512,1024]{1,0:T(8,128)(2,1)S(1)}, bf16[512,1024]{1,0:T(8,128)(2,1)S(1)}) custom-call(s32[4,32]{1,0:T(4,128)S(1)} %reshape.60.table, bf16[16,16,512]{2,1,0:T(8,128)(2,1)S(1)} %collective-permute-done.la_ref, bf16[16,16,512]{2,1,0:T(8,128)(2,1)S(1)} %collective-permute-done.1.lb_ref, ...), custom_call_target="tpu_custom_call" | custom-call | flops 1073741824 | bytes 5248000 | tf_op jit(solution)/shard_map/near_projection/pallas_call | solution.py:331
  76.3 0.5 collective-permute-done.5.far_b_ref
  76.8 3.1 %collective-permute-done.4.far_a_ref = bf16[16,16,512]{2,1,0:T(8,128)(2,1)S(1)} collective-permute-done((bf16[16,16,512]{2,1,0:T(8,128)(2,1)S(1)}, bf16[16,16,512]{2,1,0:T(8,128)(2,1)S(1)}, u32[]{:S(2)}, u32[]{:S(2)}) %collective-permute-start.4) | collective-permute-done | bytes 262176 | tf_op jit(solution)/shard_map/ppermute | solution.py:461
  79.9 6.2 %coarse_layer.1 = (bf16[32,16,512]{2,1,0:T(8,128)(2,1)}, bf16[32,16,512]{2,1,0:T(8,128)(2,1)S(1)}) custom-call(s32[4,32]{1,0:T(4,128)S(1)} %reshape.60.table, s32[64]{0:T(128)S(1)} %reshape.62.blocks, s32[8]{0:T(128)S(1)} %get-tuple-element.40.counts, bf16[512,512]{1,0:T(8,128)(2,1)S(1)} %get-tuple-element.42.pooled_ref, ...), custom_call_target="tpu_custom_call" | custom-call | flops 4000000000 | bytes 13637184 | tf_op jit(solution)/shard_map/coarse_layer/pallas_call | solution.py:331
  86.1 16.5 %all_to_all.21.coarse_ref = bf16[32,16,512]{2,1,0:T(8,128)(2,1)S(1)} all-to-all(bf16[32,16,512]{2,1,0:T(8,128)(2,1)S(1)} %get-tuple-element.46), channel_id=1, replica_groups=mesh['pts'=32,'grp'=4] {'pts'}, dimensions={0} | all-to-all | bytes 1048576 | tf_op jit(solution)/shard_map/all_to_all | solution.py:348
  102.6 6.7 %third_layer.1 = bf16[32,64,256]{2,1,0:T(8,128)(2,1)S(1)} custom-call(s32[32]{0:T(128)S(1)} %select_reduce_fusion.place, bf16[8,256,256]{2,1,0:T(8,128)(2,1)S(1)} %get-tuple-element.38.x_ref, bf16[32,16,512]{2,1,0:T(8,128)(2,1)S(1)} %all_to_all.21.coarse_ref, f32[3,256]{1,0:T(4,128)S(1)} %copy-done.4, bf16[256,768]{1,0:T(8,128)(2,1)S(1)} %get-tuple-element.47.wqkv_ref, ...), custom_call_target="tpu_custom_call" | custom-call | flops 5000000000 | bytes 6297856 | tf_op jit(solution)/shard_map/third_layer/pallas_call | solution.py:331
  109.3 20.7 %all_to_all.22.x_ref = bf16[32,64,256]{2,1,0:T(8,128)(2,1)S(1)} all-to-all(bf16[32,64,256]{2,1,0:T(8,128)(2,1)S(1)} %third_layer.1), channel_id=1, replica_groups=mesh['pts'=32,'grp'=4] {'pts'}, dimensions={0} | all-to-all | bytes 2097152 | tf_op jit(solution)/shard_map/all_to_all | solution.py:348
  130.0 1.5 %ordered.1 = bf16[32,64,256]{2,1,0:T(8,128)(2,1)} custom-call(s32[4,32]{1,0:T(4,128)S(1)} %reshape.60.table, bf16[32,64,256]{2,1,0:T(8,128)(2,1)S(1)} %all_to_all.22.x_ref), custom_call_target="tpu_custom_call" | custom-call | bytes 2098176 | tf_op jit(solution)/shard_map/ordered/pallas_call | solution.py:331
  (12 shorter events, 0.1 us)
Async XLA Ops:
  8.6 9.7 %copy-start.7 = (s32[4096]{0:T(1024)S(1)}, s32[4096]{0:T(1024)}, u32[]{:S(2)}) copy-start(s32[4096]{0:T(1024)} %rot_hbm.1) | copy-start | bytes 49156
  8.7 9.9 %copy-start.9 = (s32[1,8]{1,0:T(1,128)S(1)}, s32[1,8]{1,0:T(1,128)}, u32[]{:S(2)}) copy-start(s32[1,8]{1,0:T(1,128)} %param.15) | copy-start | bytes 100
  8.7 10.1 %copy-start.8 = (s32[1,32]{1,0:T(1,128)S(1)}, s32[1,32]{1,0:T(1,128)}, u32[]{:S(2)}) copy-start(s32[1,32]{1,0:T(1,128)} %param.14) | copy-start | bytes 388
  8.7 11.6 %copy-start.6 = (bf16[3,256,256]{2,1,0:T(8,128)(2,1)S(1)}, bf16[3,256,256]{2,1,0:T(8,128)(2,1)}, u32[]{:S(2)}) copy-start(bf16[3,256,256]{2,1,0:T(8,128)(2,1)} %wo_hbm.1) | copy-start | bytes 1179652
  8.7 26.6 %all-to-all-start = ((bf16[32,64,256]{2,1,0:T(8,128)(2,1)}), bf16[32,64,256]{2,1,0:T(8,128)(2,1)S(1)}, u32[]{:S(2)}, u32[]{:S(2)}) async-start(bf16[32,64,256]{2,1,0:T(8,128)(2,1)} %first_layer.1), calls=%async_computation | async-start | bytes 2097152 | tf_op jit(solution)/shard_map/all_to_all | solution.py:348
  18.3 17.0 %copy-start.1 = (bf16[1024,512]{1,0:T(8,128)(2,1)S(1)}, bf16[1024,512]{1,0:T(8,128)(2,1)}, u32[]{:S(2)}) copy-start(bf16[1024,512]{1,0:T(8,128)(2,1)} %pool_ref.1) | copy-start | bytes 3145732
  18.3 17.0 %copy-start.4 = (f32[3,256]{1,0:T(4,128)S(1)}, f32[3,256]{1,0:T(4,128)}, u32[]{:S(2)}) copy-start(f32[3,256]{1,0:T(4,128)} %gain_ref.1) | copy-start | bytes 9220
  42.2 26.7 %copy-start = (bf16[512,1536]{1,0:T(8,128)(2,1)S(1)}, bf16[512,1536]{1,0:T(8,128)(2,1)}, u32[]{:S(2)}) copy-start(bf16[512,1536]{1,0:T(8,128)(2,1)} %w_ref.5) | copy-start | bytes 4718596
  42.2 26.7 %copy-start.5 = (f32[512]{0:T(512)S(1)}, f32[512]{0:T(512)}, u32[]{:S(2)}) copy-start(f32[512]{0:T(512)} %param.20) | copy-start | bytes 6148
  57.5 8.1 %collective-permute-start.3 = (bf16[16,16,512]{2,1,0:T(8,128)(2,1)S(1)}, bf16[16,16,512]{2,1,0:T(8,128)(2,1)S(1)}, u32[]{:S(2)}, u32[]{:S(2)}) collective-permute-start(bf16[16,16,512]{2,1,0:T(8,128)(2,1)S(1)} %get-tuple-element.54), channel_id=1, source_target_pairs={{0,3},{1,0},{2,1},{3,2},{4,7},{5,4},{6,5},{7,6},{8,11},{9,8},{10,9... | collective-permute-start | bytes 786440 | tf_op jit(solution)/shard_map/ppermute | solution.py:449
  60.3 8.7 %collective-permute-start = (bf16[16,16,512]{2,1,0:T(8,128)(2,1)S(1)}, bf16[16,16,512]{2,1,0:T(8,128)(2,1)S(1)}, u32[]{:S(2)}, u32[]{:S(2)}) collective-permute-start(bf16[16,16,512]{2,1,0:T(8,128)(2,1)S(1)} %get-tuple-element.55), channel_id=1, source_target_pairs={{0,1},{1,2},{2,3},{3,0},{4,5},{5,6},{6,7},{7,4},{8,9},{9,10},{10,1... | collective-permute-start | bytes 786440 | tf_op jit(solution)/shard_map/ppermute | solution.py:448
  60.3 14.0 %collective-permute-start.1 = (bf16[16,16,512]{2,1,0:T(8,128)(2,1)S(1)}, bf16[16,16,512]{2,1,0:T(8,128)(2,1)S(1)}, u32[]{:S(2)}, u32[]{:S(2)}) collective-permute-start(bf16[16,16,512]{2,1,0:T(8,128)(2,1)S(1)} %get-tuple-element.54), channel_id=1, source_target_pairs={{0,1},{1,2},{2,3},{3,0},{4,5},{5,6},{6,7},{7,4},{8,9},{9,10},{10,1... | collective-permute-start | bytes 786440 | tf_op jit(solution)/shard_map/ppermute | solution.py:450
  60.3 14.0 %collective-permute-start.2 = (bf16[16,16,512]{2,1,0:T(8,128)(2,1)S(1)}, bf16[16,16,512]{2,1,0:T(8,128)(2,1)S(1)}, u32[]{:S(2)}, u32[]{:S(2)}) collective-permute-start(bf16[16,16,512]{2,1,0:T(8,128)(2,1)S(1)} %get-tuple-element.55), channel_id=1, source_target_pairs={{0,3},{1,0},{2,1},{3,2},{4,7},{5,4},{6,5},{7,6},{8,11},{9,8},{10,9... | collective-permute-start | bytes 786440 | tf_op jit(solution)/shard_map/ppermute | solution.py:451
  65.5 11.2 %collective-permute-start.5 = (bf16[16,16,512]{2,1,0:T(8,128)(2,1)S(1)}, bf16[16,16,512]{2,1,0:T(8,128)(2,1)S(1)}, u32[]{:S(2)}, u32[]{:S(2)}) collective-permute-start(bf16[16,16,512]{2,1,0:T(8,128)(2,1)S(1)} %collective-permute-done.3.rb_ref), channel_id=1, source_target_pairs={{0,3},{1,0},{2,1},{3,2},{4,7},{5,4},{6,5},{7,6},{8,11},{9,8},{10,9... | collective-permute-start | bytes 786440 | tf_op jit(solution)/shard_map/ppermute | solution.py:462
  69.0 11.0 %collective-permute-start.4 = (bf16[16,16,512]{2,1,0:T(8,128)(2,1)S(1)}, bf16[16,16,512]{2,1,0:T(8,128)(2,1)S(1)}, u32[]{:S(2)}, u32[]{:S(2)}) collective-permute-start(bf16[16,16,512]{2,1,0:T(8,128)(2,1)S(1)} %collective-permute-done.la_ref), channel_id=1, source_target_pairs={{0,1},{1,2},{2,3},{3,0},{4,5},{5,6},{6,7},{7,4},{8,9},{9,10},{10,1... | collective-permute-start | bytes 786440 | tf_op jit(solution)/shard_map/ppermute | solution.py:461
  70.6 9.3 %copy-start.3 = (bf16[512,512]{1,0:T(8,128)(2,1)S(1)}, bf16[512,512]{1,0:T(8,128)(2,1)}, u32[]{:S(2)}) copy-start(bf16[512,512]{1,0:T(8,128)(2,1)} %wo_ref.1) | copy-start | bytes 1572868
  79.9 22.7 %copy-start.2 = (bf16[512,1024]{1,0:T(8,128)(2,1)S(1)}, bf16[512,1024]{1,0:T(8,128)(2,1)}, u32[]{:S(2)}) copy-start(bf16[512,1024]{1,0:T(8,128)(2,1)} %unpool_ref.1) | copy-start | bytes 3145732
